TPU v7x, 32 devices: a whole 2x2x4 slice. The times are simulated.
32 devices in a mesh: user: 4 (over x, core), heads: 2 (over y), ctx: 4 (over z).
Axes of the slice: x: 2, y: 2, z: 4, core: 2. Of those that a mesh axis runs over, the one named last changes fastest.
Arguments:
- keys: bfloat16 [65536, 512], P(('user', 'ctx'), 'heads'), parts along dimension 0, may hold values from -6 to 6
- values: bfloat16 [65536, 512], P(('user', 'ctx'), 'heads'), parts along dimension 0, may hold values from -6 to 6
- queries: bfloat16 [4, 12288, 128], P('heads', ('user', 'ctx')), parts along dimension 1, may hold values from -240 to 240
- positions: int32 [12288], P(('user', 'ctx')), parts along dimension 0, may hold values from 0 to 16383
Outputs:
- attended: bfloat16 [4, 12288, 128], P('heads', ('user', 'ctx')), parts along dimension 1
There are 4 independent parts, one for each index of `user`. A program takes and returns all parts, laid end to end along the dimension named above; each array names one. Nothing has to cross between parts.
All inputs are finite; a program needn't handle non-finite values.
Results may differ from a plain program's by a relative error of at most 0.008.
The roundings to bfloat16 on the way count: a program that leaves them out, or rounds other values in their place, can miss the bound.
Values may be sent and summed in bfloat16 or wider, within the bound.
A program may use at most 128 MiB of HBM per device.

v0:
```python
import functools
import math

import jax
import jax.numpy as jnp
import numpy as np
from jax import lax
from jax.experimental import pallas as pl
from jax.experimental.pallas import tpu as pltpu
from jax.sharding import PartitionSpec as P

OUTER = 128


def split_two(matrix):
    high = matrix.astype(jnp.bfloat16)
    low = (matrix - np.asarray(high).astype(np.float64)).astype(jnp.bfloat16)
    return high, low


@functools.lru_cache(maxsize=None)
def stages(length):
    outer = OUTER
    inner = length // outer
    step = inner // 2
    a = np.arange(outer)
    c = np.arange(outer)
    turn = 2 * outer
    angle = np.pi / outer * ((c[:, None] * a[None, :]) % turn)
    alternate = np.where(a % 2 == 0, 1.0, -1.0)
    first = np.stack([np.cos(angle), -np.sin(angle)], axis=1)
    first[0, 1] = alternate
    d = np.arange(length // 2 // turn)
    k = np.concatenate([c[:, None] + turn * d, (turn - c[:, None]) % turn + turn * d], axis=1)
    k[0, d.size :] = outer + turn * d
    sign = np.concatenate([np.ones(d.size), -np.ones(d.size)])
    b = np.arange(inner)
    q = np.arange(step)
    theta = np.pi / (2 * length) * ((k[:, :, None] * (2 * b + 1)) % (4 * length))
    phi = np.pi / length * ((k[:, None, :] * (2 * q + 1)[:, None]) % (2 * length))
    forward = np.stack([np.cos(theta), np.sin(theta) * sign[None, :, None]], axis=2)
    weight = np.where(k == 0, 1.0, 2.0) / length
    back = np.stack([np.cos(phi), np.sin(phi) * sign], axis=1) * weight[:, None, None, :]
    half = d.size
    forward[0, :half, 1] = 0.0
    forward[0, half:, 1] = np.cos(theta[0, half:])
    forward[0, half:, 0] = 0.0
    back[0, 1, :, :half] = 0.0
    back[0, 1, :, half:] = np.cos(phi[0, :, half:]) * weight[0, half:]
    back[0, 0, :, half:] = 0.0
    middle = back.reshape(outer, 2 * step, 2 * half) @ forward.reshape(outer, 2 * half, 2 * inner)
    last = first.transpose(2, 0, 1).reshape(outer, 2 * outer)
    return first.reshape(2 * outer, outer), middle, last


def compress(signal):
    length, columns = signal.shape
    outer, inner = OUTER, length // OUTER
    first, middle, last = stages(length)
    first_high, first_low = split_two(first)
    flat = signal.reshape(outer, inner * columns)
    one = jnp.dot(first_high, flat, preferred_element_type=jnp.float32) + jnp.dot(
        first_low, flat, preferred_element_type=jnp.float32
    )
    one = one.reshape(outer, 2 * inner, columns)
    two = jnp.einsum(
        "cob,cbl->col", jnp.asarray(middle.astype(np.float32)), one, precision=lax.Precision.HIGH
    )
    three = jnp.dot(
        jnp.asarray(last.astype(np.float32)),
        two.reshape(2 * outer, inner // 2 * columns),
        precision=lax.Precision.HIGH,
    )
    return three.reshape(length // 2, columns).astype(jnp.bfloat16)

GAP = 8


def strict_dot(left, right):
    rows, columns = left.shape[0] // 2, right.shape[1]
    high = right.astype(jnp.bfloat16)
    low = (right - high.astype(jnp.float32)).astype(jnp.bfloat16)
    both = jnp.dot(
        left, jnp.concatenate([high, low], axis=1), preferred_element_type=jnp.float32
    )
    return both[:rows, :columns] + (both[:rows, columns:] + both[rows:, :columns])


def compress_kernel(
    inner,
    odd_ref,
    x_ref,
    first_ref,
    middle_ref,
    last_ref,
    coarse_ref,
    fine_ref,
    keep_ref,
    send_one_ref,
    send_two_ref,
    wide_ref,
    one_ref,
):
    outer = OUTER
    step = inner // 2
    columns = x_ref.shape[1]
    here = pl.program_id(0)
    steps = pl.num_programs(0)
    per_step = middle_ref.shape[0]
    x_pitch = inner + GAP
    one_pitch = 2 * outer + GAP
    two_pitch = step + GAP

    @pl.when(here == 0)
    def _():
        def widen(a, carry):
            source = pl.multiple_of(a * inner, inner)
            wide_ref[pl.ds(pl.multiple_of(a * x_pitch, GAP), inner), :] = x_ref[
                pl.ds(source, inner), :
            ].astype(jnp.float32)
            return carry

        lax.fori_loop(0, outer, widen, 0, unroll=4)

        def stage_one(pair, carry):
            x = jnp.concatenate(
                [
                    wide_ref[pl.ds(2 * pair + i, outer, stride=x_pitch), :].astype(jnp.bfloat16)
                    for i in range(2)
                ],
                axis=1,
            )
            z = jnp.dot(
                first_ref[...],
                jnp.concatenate([x, x], axis=0),
                preferred_element_type=jnp.float32,
            )
            for i in range(2):
                start = pl.multiple_of((2 * pair + i) * one_pitch, GAP)
                one_ref[pl.ds(start, 2 * outer), :] = z[:, i * columns : (i + 1) * columns]
            return carry

        lax.fori_loop(0, inner // 2, stage_one, 0, unroll=4)

    for i in range(per_step):
        c = here * per_step + i
        z = jnp.concatenate(
            [
                one_ref[pl.ds(2 * c, inner, stride=one_pitch), :],
                one_ref[pl.ds(2 * c + 1, inner, stride=one_pitch), :],
            ],
            axis=0,
        )
        v = strict_dot(middle_ref[i], z)
        for part in range(2):
            wide_ref[pl.ds(pl.multiple_of((2 * c + part) * two_pitch, GAP), step), :] = v[
                part * step : (part + 1) * step
            ]

    @pl.when(here == steps - 1)
    def _():
        def stage_three(out_ref, offset):
            def one(i, carry):
                q = offset + i
                v = wide_ref[pl.ds(q, 2 * outer, stride=two_pitch), :]
                y = strict_dot(last_ref[...], v).astype(jnp.bfloat16).astype(jnp.float32)
                front = lax.broadcasted_iota(jnp.int32, y.shape, 1) < columns // 2
                cos_p, sin_p = coarse_ref[0], coarse_ref[1]
                cos_q, sin_q = fine_ref[0, pl.ds(q, 1), :], fine_ref[1, pl.ds(q, 1), :]
                sine = sin_p * cos_q + cos_p * sin_q
                other = pltpu.roll(y, columns // 2, 1)
                turned = y * (cos_p * cos_q - sin_p * sin_q) + other * jnp.where(
                    front, -sine, sine
                )
                out_ref[pl.ds(pl.multiple_of(i * outer, outer), outer), :] = turned.astype(
                    out_ref.dtype
                )
                return carry

            lax.fori_loop(0, out_ref.shape[0] // outer, one, 0, unroll=4)

        odd = odd_ref[0]
        stage_three(send_one_ref, (1 - odd) * (step // 2))
        stage_three(send_two_ref, (1 - odd) * (step // 2) + step // 4)
        stage_three(keep_ref, odd * (step // 2))


def turns(places, width):
    angles = places[:, None] * inverse_freq(width)[None, :]
    cosine, sine = jnp.cos(angles), jnp.sin(angles)
    return jnp.stack(
        [jnp.concatenate([cosine, cosine], axis=1), jnp.concatenate([sine, sine], axis=1)]
    )


def compress_rows(signal, odd):
    length, columns = signal.shape
    outer, inner = OUTER, length // OUTER
    step = inner // 2
    first, middle, last = stages(length)
    first_pair = np.concatenate(split_two(first), axis=1)
    middle_pair = np.concatenate(split_two(middle), axis=1)
    last_pair = np.concatenate(split_two(last), axis=0)
    turned = (1 - odd).astype(jnp.float32)
    coarse = turns(jnp.arange(outer).astype(jnp.float32) * step * turned, columns)
    fine = turns(jnp.arange(step).astype(jnp.float32) * turned, columns)
    per_step = 8
    rows_wide = max(outer * (inner + GAP), 2 * outer * (step + GAP))
    once = pl.BlockSpec(memory_space=pltpu.VMEM)
    half = jax.ShapeDtypeStruct((length // 4, columns), jnp.bfloat16)
    quarter = jax.ShapeDtypeStruct((length // 8, columns), jnp.bfloat16)
    return pl.pallas_call(
        functools.partial(compress_kernel, inner),
        grid=(outer // per_step,),
        in_specs=[
            pl.BlockSpec(memory_space=pltpu.SMEM),
            once,
            once,
            pl.BlockSpec((per_step, 2 * inner, 2 * inner), lambda i: (i, 0, 0)),
            once,
            once,
            once,
        ],
        out_specs=[once, once, once],
        out_shape=[half, quarter, quarter],
        scratch_shapes=[
            pltpu.VMEM((rows_wide, columns), jnp.float32),
            pltpu.VMEM((inner * (2 * outer + GAP), columns), jnp.float32),
        ],
        cost_estimate=pl.CostEstimate(
            flops=64 * length * outer * columns, bytes_accessed=16 * length * columns, transcendentals=0
        ),
    )(odd.reshape(1), signal, first_pair, middle_pair, last_pair, coarse, fine)


def inverse_freq(width):
    return jnp.exp(jnp.arange(width // 2).astype(jnp.float32) * (-2.0 * math.log(500000.0) / width))


def rotate_rows(block, places):
    width = block.shape[-1]
    half = width // 2
    angles = places[:, None] * inverse_freq(width)[None, :]
    cosine = jnp.cos(angles)
    sine = jnp.sin(angles)
    first = block[..., :half]
    second = block[..., half:]
    return jnp.concatenate(
        [first * cosine - second * sine, second * cosine + first * sine], axis=-1
    )


def attend_kernel(chunk, scale, resume, finish, swap_ref, q_ref, k_ref, v_ref, *refs):
    q = q_ref[0]
    swap = swap_ref[0] == 1
    rows, width = q.shape
    factor = scale * math.log2(math.e)
    if resume:
        accum = refs[0][0]
        best = refs[1][0][:, :1]
        total = refs[2][0][:, :1]
        refs = refs[3:]
    else:
        best = jnp.full((rows, 1), -jnp.inf, jnp.float32)
        total = jnp.zeros((rows, 1), jnp.float32)
        accum = jnp.zeros((rows, width), jnp.float32)
    tokens = k_ref.shape[1]
    for start in range(0, tokens, chunk):
        one = k_ref[0, start : start + chunk, :]
        two = v_ref[0, start : start + chunk, :]
        k, v = jnp.where(swap, two, one), jnp.where(swap, one, two)
        scores = lax.dot_general(
            q, k, (((1,), (1,)), ((), ())), preferred_element_type=jnp.float32
        )
        fresh = jnp.maximum(best, jnp.max(scores, axis=1, keepdims=True))
        expo = jnp.exp2((scores - fresh) * factor)
        shrink = jnp.exp2((best - fresh) * factor)
        total = total * shrink + jnp.sum(expo, axis=1, keepdims=True)
        accum = accum * shrink + jnp.dot(
            expo.astype(jnp.bfloat16), v, preferred_element_type=jnp.float32
        )
        best = fresh
    if finish:
        refs[0][0] = (accum / total).astype(refs[0].dtype)
        refs[1][0] = jnp.broadcast_to(best * factor + jnp.log2(total), (rows, 8))
    else:
        refs[0][0] = accum
        refs[1][0] = jnp.broadcast_to(best, (rows, 8))
        refs[2][0] = jnp.broadcast_to(total, (rows, 8))


def attend(queries, keys, values, swap, part=0, parts=1, state=None):
    groups, rows, width = queries.shape
    heads, tokens, _ = values.shape
    per_head = groups // heads
    block = math.gcd(rows, 768)
    chunk = math.gcd(tokens, 1024)
    scale = 1.0 / math.sqrt(width)
    finish = part == parts - 1
    wide = pl.BlockSpec((1, block, width), lambda g, i: (g, i, 0))
    thin = pl.BlockSpec((1, block, 8), lambda g, i: (g, i, 0))
    thin_shape = jax.ShapeDtypeStruct((groups, rows, 8), jnp.float32)
    state = () if state is None else tuple(state)
    wide_type = jnp.bfloat16 if finish else jnp.float32
    return pl.pallas_call(
        functools.partial(attend_kernel, chunk, scale, bool(state), finish),
        grid=(groups, rows // block),
        in_specs=[
            pl.BlockSpec(memory_space=pltpu.SMEM),
            wide,
            pl.BlockSpec((1, tokens, width), lambda g, i: (g // per_head, part, 0)),
            pl.BlockSpec((1, tokens, width), lambda g, i: (g // per_head, 0, 0)),
        ]
        + ([wide, thin, thin] if state else []),
        out_specs=[wide, thin] if finish else [wide, thin, thin],
        out_shape=[jax.ShapeDtypeStruct((groups, rows, width), wide_type), thin_shape]
        + ([] if finish else [thin_shape]),
        cost_estimate=pl.CostEstimate(
            flops=8 * groups * rows * tokens * width,
            bytes_accessed=4 * groups * rows * width * 2,
            transcendentals=groups * rows * tokens,
        ),
    )(swap.reshape(1), queries, keys, values, *state)


def by_pairs(keys, values, queries, positions, count):
    heads, rows, width = queries.shape
    me = lax.axis_index("ctx")
    odd = (me % 2).astype(jnp.int32)
    pieces = []
    for head in range(heads):
        pieces.append(keys[:, head * width : (head + 1) * width])
        pieces.append(values[:, head * width : (head + 1) * width])
    mine = lax.all_to_all(jnp.stack(pieces), "ctx", split_axis=0, concat_axis=0, tiled=True)
    rotated = rotate_rows(queries.astype(jnp.float32), positions.astype(jnp.float32)).astype(
        jnp.bfloat16
    )
    asked = lax.all_to_all(
        jnp.repeat(rotated, 2, axis=0), "ctx", split_axis=0, concat_axis=0, tiled=True
    )
    keep, *sends = compress_rows(mine.reshape(-1, width), odd)
    pairs = [(i, i ^ 1) for i in range(count)]
    others = [lax.ppermute(send, "ctx", pairs) for send in sends]
    state = None
    for part, other in enumerate(others):
        state = attend(asked, keep[None], other[None], odd, part, len(others), state)
    part, lse = state
    lse = lse[:, :, 0].reshape(count, rows // width, width)
    top = lax.reduce_precision(lse, 8, 7)
    rest = lse - top
    mid = lax.reduce_precision(rest, 8, 7)
    last = (rest - mid).astype(jnp.bfloat16)
    top, mid = top.astype(jnp.bfloat16), mid.astype(jnp.bfloat16)
    sent = lax.all_to_all(
        jnp.concatenate([part, top, mid, last], axis=1),
        "ctx",
        split_axis=0,
        concat_axis=0,
        tiled=True,
    )
    got = sent[:, :rows].astype(jnp.float32).reshape(heads, 2, rows, width)
    logs = jnp.sum(
        sent[:, rows:].astype(jnp.float32).reshape(heads, 2, 3, rows), axis=2
    )
    share = jax.nn.sigmoid((logs[:, 0] - logs[:, 1]) * math.log(2.0))[..., None]
    return (got[:, 0] * share + got[:, 1] * (1.0 - share)).astype(jnp.bfloat16)


def by_columns(keys, values, queries, positions):
    key_parts = lax.all_to_all(keys, "ctx", split_axis=1, concat_axis=0, tiled=True)
    value_parts = lax.all_to_all(values, "ctx", split_axis=1, concat_axis=0, tiled=True)
    heads, rows, width = queries.shape
    per_device = key_parts.shape[1]
    compact = compress(jnp.concatenate([key_parts, value_parts], axis=1))
    rotated = rotate_rows(queries.astype(jnp.float32), positions.astype(jnp.float32)).astype(
        jnp.bfloat16
    )
    whole = lax.all_gather(compact.T, "ctx", axis=0, tiled=True)
    tokens = whole.shape[1]
    shaped = whole.reshape(-1, 2, per_device, tokens)
    key_rows = shaped[:, 0].reshape(heads, width, tokens).swapaxes(1, 2)
    value_rows = shaped[:, 1].reshape(heads, width, tokens).swapaxes(1, 2)
    places = jnp.arange(tokens).astype(jnp.float32)
    ready = rotate_rows(key_rows.astype(jnp.float32), places).astype(jnp.bfloat16)
    return attend(rotated, ready, value_rows, jnp.zeros((), jnp.int32))[0]


def solution(mesh):
    count = mesh.shape["ctx"]

    def on_device(keys, values, queries, positions):
        heads, rows, width = queries.shape
        if count == 2 * heads and rows % width == 0:
            return by_pairs(keys, values, queries, positions, count)
        return by_columns(keys, values, queries, positions)

    return jax.shard_map(
        on_device,
        mesh=mesh,
        in_specs=(
            P(("user", "ctx"), "heads"),
            P(("user", "ctx"), "heads"),
            P("heads", ("user", "ctx"), None),
            P(("user", "ctx")),
        ),
        out_specs=P("heads", ("user", "ctx"), None),
        check_vma=False,
    )
```

profile of v0, /device:TPU:0, one launch (start us, length us, event | category | flops | bytes accessed | tf_op | source)
XLA Modules:
  0.0 214.4 jit_solution(9811191890090881270)
XLA Ops:
  0.0 2.4 %slice_bitcast_fusion.2 = (bf16[1,4096,128]{2,1,0:T(8,128)(2,1)S(1)}, bf16[1,4096,128]{2,1,0:T(8,128)(2,1)S(1)}, bf16[1,4096,128]{2,1,0:T(8,128)(2,1)S(1)}, bf16[1,4096,128]{2,1,0:T(8,128)(2,1)S(1)}) fusion(bf16[4096,256]{1,0:T(8,128)(2,1)} %param.8, bf16[4096,256]{1,0:T(8,128)(2,1)} %param.7), kind=kLoop, calls=%fused_computation.4 | loop fusion | bytes 8388608 | tf_op jit(solution)/shard_map/stack | solution.py:334
  2.4 2.3 %pad_maximum_fusion = bf16[4,4096,128]{2,1,0:T(8,128)(2,1)} fusion(bf16[1,4096,128]{2,1,0:T(8,128)(2,1)S(1)} %get-tuple-element.24, bf16[1,4096,128]{2,1,0:T(8,128)(2,1)S(1)} %get-tuple-element.36, bf16[1,4096,128]{2,1,0:T(8,128)(2,1)S(1)} %get-tuple-element.23, bf16[1,4096,128]{2,1,0:T(8,128)(2,1)S(1)} %get-tuple-element.37), kind=kLoop, calls=%fused_computation | loop fusion | flops 6291456 | bytes 8388608 | tf_op jit(solution)/shard_map/stack | solution.py:334
  4.7 6.5 %all-to-all-start.1 = ((bf16[4,4096,128]{2,1,0:T(8,128)(2,1)}), bf16[4,4096,128]{2,1,0:T(8,128)(2,1)}, u32[]{:S(2)}, u32[]{:S(2)}) async-start(bf16[4,4096,128]{2,1,0:T(8,128)(2,1)} %pad_maximum_fusion), calls=%async_computation.1 | async-start | bytes 8388608 | tf_op jit(solution)/shard_map/all_to_all | solution.py:334
  11.3 0.2 multiply_cosine_fusion.2
  11.6 0.6 pad_maximum_fusion.4.fine_ref
  12.2 0.3 multiply_cosine_fusion.1
  12.6 0.7 pad_maximum_fusion.3.coarse_ref
  13.3 1.4 multiply_cosine_fusion
  14.7 0.4 subtract_convert_fusion
  15.1 0.2 pad_maximum_fusion.2
  15.4 89.2 %all-to-all-done.1 = bf16[4,4096,128]{2,1,0:T(8,128)(2,1)} async-done(((bf16[4,4096,128]{2,1,0:T(8,128)(2,1)}), bf16[4,4096,128]{2,1,0:T(8,128)(2,1)}, u32[]{:S(2)}, u32[]{:S(2)}) %all-to-all-start.1) | async-done | bytes 4194336 | tf_op jit(solution)/shard_map/all_to_all | solution.py:334
  104.6 1.0 broadcast_in_dim.8
  105.6 3.7 %all-to-all-start = ((bf16[4,768,128]{2,1,0:T(8,128)(2,1)}), bf16[4,768,128]{2,1,0:T(8,128)(2,1)S(1)}, u32[]{:S(2)}, u32[]{:S(2)}) async-start(bf16[4,768,128]{2,1,0:T(8,128)(2,1)} %bitcast.1), calls=%async_computation | async-start | bytes 1572864 | tf_op jit(solution)/shard_map/all_to_all | solution.py:338
  109.3 29.9 %shard_map.73 = (bf16[4096,128]{1,0:T(8,128)(2,1)}, bf16[2048,128]{1,0:T(8,128)(2,1)}, bf16[2048,128]{1,0:T(8,128)(2,1)}) custom-call(s32[1]{0:T(128)} %bitcast.odd_ref.swap_ref, bf16[16384,128]{1,0:T(8,128)(2,1)} %bitcast.6.x_ref, bf16[256,256]{1,0:T(8,128)(2,1)} %constant.35.clone.first_ref, bf16[128,256,256]{2,1,0:T(8,128)(2,1)} %constant.36.clone.middle_ref, ...), custom_call_target="tpu_custom_call" | custom-call | flops 17179869184 | bytes 33554432 | tf_op jit(solution)/shard_map/pallas_call | solution.py:212
  139.1 1.8 collective-permute-start.1
  140.9 0.2 collective-permute-start
  141.2 13.0 %collective-permute-done.1 = bf16[2048,128]{1,0:T(8,128)(2,1)S(1)} collective-permute-done((bf16[2048,128]{1,0:T(8,128)(2,1)}, bf16[2048,128]{1,0:T(8,128)(2,1)S(1)}, u32[]{:S(2)}, u32[]{:S(2)}) %collective-permute-start.1) | collective-permute-done | bytes 524320 | tf_op jit(solution)/shard_map/ppermute | solution.py:343
  154.2 0.8 copy-done.5
  155.0 11.5 %shard_map.74 = (f32[4,768,128]{2,1,0:T(8,128)}, f32[4,768,8]{2,1,0:T(8,128)}, f32[4,768,8]{2,1,0:T(8,128)}) custom-call(s32[1]{0:T(128)} %bitcast.odd_ref.swap_ref, bf16[4,768,128]{2,1,0:T(8,128)(2,1)} %copy-done, bf16[1,4096,128]{2,1,0:T(8,128)(2,1)} %bitcast.51, bf16[1,2048,128]{2,1,0:T(8,128)(2,1)} %bitcast.50), custom_call_target="tpu_custom_call" | custom-call | flops 6442450944 | bytes 3145728 | tf_op jit(solution)/shard_map/pallas_call | solution.py:305
  166.5 0.8 copy-done.4
  167.3 22.5 %shard_map.75 = (bf16[4,768,128]{2,1,0:T(8,128)(2,1)}, f32[4,768,8]{2,1,0:T(8,128)}) custom-call(s32[1]{0:T(128)} %bitcast.odd_ref.swap_ref, bf16[4,768,128]{2,1,0:T(8,128)(2,1)} %copy-done, bf16[1,4096,128]{2,1,0:T(8,128)(2,1)} %bitcast.52, bf16[1,2048,128]{2,1,0:T(8,128)(2,1)} %bitcast.49, f32[4,768,128]{2,1,0:T(8,128)} %get-tuple-element.16.refs_0_, ...), custom_call_target="tpu_custom_call" | custom-call | flops 6442450944 | bytes 3145728 | tf_op jit(solution)/shard_map/pallas_call | solution.py:305
  189.8 2.0 slice_reduce_fusion
  191.9 21.0 %all_to_all.15 = bf16[4,786,128]{2,1,0:T(8,128)(2,1)S(1)} all-to-all(bf16[4,786,128]{2,1,0:T(8,128)(2,1)S(1)} %pad_maximum_fusion.1), channel_id=1, replica_groups=mesh['user'=4,'heads'=2,'ctx'=4] {'ctx'}, dimensions={0} | all-to-all | bytes 1609728 | tf_op jit(solution)/shard_map/all_to_all | solution.py:354
  213.2 1.2 fusion.2
  (30 shorter events, 0.6 us)
Async XLA Ops:
  4.7 6.5 %copy-start.3 = (s32[768]{0:T(1024)S(1)}, s32[768]{0:T(1024)}, u32[]{:S(2)}) copy-start(s32[768]{0:T(1024)} %param.10) | copy-start | bytes 9220
  4.7 6.5 %copy-start.2 = (bf16[2,768,128]{2,1,0:T(8,128)(2,1)S(1)}, bf16[2,768,128]{2,1,0:T(8,128)(2,1)}, u32[]{:S(2)}) copy-start(bf16[2,768,128]{2,1,0:T(8,128)(2,1)} %param.9) | copy-start | bytes 1179652
  4.7 99.9 %all-to-all-start.1 = ((bf16[4,4096,128]{2,1,0:T(8,128)(2,1)}), bf16[4,4096,128]{2,1,0:T(8,128)(2,1)}, u32[]{:S(2)}, u32[]{:S(2)}) async-start(bf16[4,4096,128]{2,1,0:T(8,128)(2,1)} %pad_maximum_fusion), calls=%async_computation.1 | async-start | bytes 8388608 | tf_op jit(solution)/shard_map/all_to_all | solution.py:334
  105.6 35.6 %all-to-all-start = ((bf16[4,768,128]{2,1,0:T(8,128)(2,1)}), bf16[4,768,128]{2,1,0:T(8,128)(2,1)S(1)}, u32[]{:S(2)}, u32[]{:S(2)}) async-start(bf16[4,768,128]{2,1,0:T(8,128)(2,1)} %bitcast.1), calls=%async_computation | async-start | bytes 1572864 | tf_op jit(solution)/shard_map/all_to_all | solution.py:338
  139.1 15.0 %collective-permute-start.1 = (bf16[2048,128]{1,0:T(8,128)(2,1)}, bf16[2048,128]{1,0:T(8,128)(2,1)S(1)}, u32[]{:S(2)}, u32[]{:S(2)}) collective-permute-start(bf16[2048,128]{1,0:T(8,128)(2,1)} %get-tuple-element.15), channel_id=1, source_target_pairs={{0,1},{1,0},{2,3},{3,2},{4,5},{5,4},{6,7},{7,6},{8,9},{9,8},{10,11... | collective-permute-start | bytes 1572872 | tf_op jit(solution)/shard_map/ppermute | solution.py:343
  140.9 25.6 %collective-permute-start = (bf16[2048,128]{1,0:T(8,128)(2,1)}, bf16[2048,128]{1,0:T(8,128)(2,1)S(1)}, u32[]{:S(2)}, u32[]{:S(2)}) collective-permute-start(bf16[2048,128]{1,0:T(8,128)(2,1)} %get-tuple-element.14), channel_id=1, source_target_pairs={{0,1},{1,0},{2,3},{3,2},{4,5},{5,4},{6,7},{7,6},{8,9},{9,8},{10,11... | collective-permute-start | bytes 1572872 | tf_op jit(solution)/shard_map/ppermute | solution.py:343
  141.2 13.0 %copy-start = (bf16[4,768,128]{2,1,0:T(8,128)(2,1)}, bf16[4,768,128]{2,1,0:T(8,128)(2,1)S(1)}, u32[]{:S(2)}) copy-start(bf16[4,768,128]{2,1,0:T(8,128)(2,1)S(1)} %all-to-all-done.q_ref) | copy-start | bytes 2359300
  154.2 0.8 copy-start.5
  166.5 0.8 copy-start.4
  189.8 2.0 copy-start.1
where the time goes:
time: 215 us; the launch traced here: 214 us
  waiting for transfers between devices  102 us (47%)
  Pallas kernels  63.9 us (30%)
  blocking collectives  21 us (10%)
  starting transfers between devices  12.2 us (6%)
  other arithmetic  7.81 us (4%)
  local copies, waits for them, and re-layouts  7.1 us (3%)
    all_to_all x1, waiting for transfers between devices, by_pairs(): lax.all_to_all(jnp.stack(pieces), 'ctx', split_axis=0, concat_axis=0, til...  89.2 us
    pallas_call x2, Pallas kernels, attend(): pl.pallas_call(functools.partial(attend_kernel, chunk, scale, bool(state)...  34 us
    pallas_call x1, Pallas kernels, compress_rows(): pl.pallas_call(functools.partial(compress_kernel, inner), grid=(outer //...  29.9 us
    all_to_all x1, blocking collectives, by_pairs(): lax.all_to_all(jnp.concatenate([part, top, mid, last], axis=1), 'ctx', sp...  21 us
    ppermute x2, waiting for transfers between devices, by_pairs(): others = [lax.ppermute(send, 'ctx', pairs) for send in sends]  13 us
    all_to_all x1, starting transfers between devices, by_pairs(): lax.all_to_all(jnp.stack(pieces), 'ctx', split_axis=0, concat_axis=0, til...  6.48 us
  transfers between devices with their start and end apart: 4, of which 2 were waited for; matrix products, arithmetic and copies ran while one was open for 2% of the time, Pallas kernels for 19%

commit v1 on v0

v1 whole, which is shorter than its diff:
```python
import functools
import math

import jax
import jax.numpy as jnp
import numpy as np
from jax import lax
from jax.experimental import pallas as pl
from jax.experimental.pallas import tpu as pltpu
from jax.sharding import PartitionSpec as P

OUTER = 128
PARTS = 4
ORDER = 64
BLOCK = 256
MESH = pl.DeviceIdType.MESH


def split_two(matrix):
    high = matrix.astype(jnp.bfloat16)
    low = (matrix - np.asarray(high).astype(np.float64)).astype(jnp.bfloat16)
    return high, low


@functools.lru_cache(maxsize=None)
def stages(length):
    outer = OUTER
    inner = length // outer
    step = inner // 2
    a = np.arange(outer)
    c = np.arange(outer)
    turn = 2 * outer
    angle = np.pi / outer * ((c[:, None] * a[None, :]) % turn)
    alternate = np.where(a % 2 == 0, 1.0, -1.0)
    first = np.stack([np.cos(angle), -np.sin(angle)], axis=1)
    first[0, 1] = alternate
    d = np.arange(length // 2 // turn)
    k = np.concatenate([c[:, None] + turn * d, (turn - c[:, None]) % turn + turn * d], axis=1)
    k[0, d.size :] = outer + turn * d
    sign = np.concatenate([np.ones(d.size), -np.ones(d.size)])
    b = np.arange(inner)
    q = np.arange(step)
    theta = np.pi / (2 * length) * ((k[:, :, None] * (2 * b + 1)) % (4 * length))
    phi = np.pi / length * ((k[:, None, :] * (2 * q + 1)[:, None]) % (2 * length))
    forward = np.stack([np.cos(theta), np.sin(theta) * sign[None, :, None]], axis=2)
    weight = np.where(k == 0, 1.0, 2.0) / length
    back = np.stack([np.cos(phi), np.sin(phi) * sign], axis=1) * weight[:, None, None, :]
    half = d.size
    forward[0, :half, 1] = 0.0
    forward[0, half:, 1] = np.cos(theta[0, half:])
    forward[0, half:, 0] = 0.0
    back[0, 1, :, :half] = 0.0
    back[0, 1, :, half:] = np.cos(phi[0, :, half:]) * weight[0, half:]
    back[0, 0, :, half:] = 0.0
    middle = back.reshape(outer, 2 * step, 2 * half) @ forward.reshape(outer, 2 * half, 2 * inner)
    last = first.transpose(2, 0, 1).reshape(outer, 2 * outer)
    return first.reshape(2 * outer, outer), middle, last


def compress(signal):
    length, columns = signal.shape
    outer, inner = OUTER, length // OUTER
    first, middle, last = stages(length)
    first_high, first_low = split_two(first)
    flat = signal.reshape(outer, inner * columns)
    one = jnp.dot(first_high, flat, preferred_element_type=jnp.float32) + jnp.dot(
        first_low, flat, preferred_element_type=jnp.float32
    )
    one = one.reshape(outer, 2 * inner, columns)
    two = jnp.einsum(
        "cob,cbl->col", jnp.asarray(middle.astype(np.float32)), one, precision=lax.Precision.HIGH
    )
    three = jnp.dot(
        jnp.asarray(last.astype(np.float32)),
        two.reshape(2 * outer, inner // 2 * columns),
        precision=lax.Precision.HIGH,
    )
    return three.reshape(length // 2, columns).astype(jnp.bfloat16)

def strict_dot(left, right):
    rows, columns = left.shape[0] // 2, right.shape[1]
    high = right.astype(jnp.bfloat16)
    low = (right - high.astype(jnp.float32)).astype(jnp.bfloat16)
    both = jnp.dot(
        left, jnp.concatenate([high, low], axis=1), preferred_element_type=jnp.float32
    )
    return both[:rows, :columns] + (both[:rows, columns:] + both[rows:, :columns])


def inverse_freq(width):
    return jnp.exp(jnp.arange(width // 2).astype(jnp.float32) * (-2.0 * math.log(500000.0) / width))


def rotate_rows(block, places):
    width = block.shape[-1]
    half = width // 2
    angles = places[:, None] * inverse_freq(width)[None, :]
    cosine = jnp.cos(angles)
    sine = jnp.sin(angles)
    first = block[..., :half]
    second = block[..., half:]
    return jnp.concatenate(
        [first * cosine - second * sine, second * cosine + first * sine], axis=-1
    )


def attend_kernel(chunk, scale, resume, finish, swap_ref, q_ref, k_ref, v_ref, *refs):
    q = q_ref[0]
    swap = swap_ref[0] == 1
    rows, width = q.shape
    factor = scale * math.log2(math.e)
    if resume:
        accum = refs[0][0]
        best = refs[1][0][:, :1]
        total = refs[2][0][:, :1]
        refs = refs[3:]
    else:
        best = jnp.full((rows, 1), -jnp.inf, jnp.float32)
        total = jnp.zeros((rows, 1), jnp.float32)
        accum = jnp.zeros((rows, width), jnp.float32)
    tokens = k_ref.shape[1]
    for start in range(0, tokens, chunk):
        one = k_ref[0, start : start + chunk, :]
        two = v_ref[0, start : start + chunk, :]
        k, v = jnp.where(swap, two, one), jnp.where(swap, one, two)
        scores = lax.dot_general(
            q, k, (((1,), (1,)), ((), ())), preferred_element_type=jnp.float32
        )
        fresh = jnp.maximum(best, jnp.max(scores, axis=1, keepdims=True))
        expo = jnp.exp2((scores - fresh) * factor)
        shrink = jnp.exp2((best - fresh) * factor)
        total = total * shrink + jnp.sum(expo, axis=1, keepdims=True)
        accum = accum * shrink + jnp.dot(
            expo.astype(jnp.bfloat16), v, preferred_element_type=jnp.float32
        )
        best = fresh
    if finish:
        refs[0][0] = (accum / total).astype(refs[0].dtype)
        refs[1][0] = jnp.broadcast_to(best * factor + jnp.log2(total), (rows, 8))
    else:
        refs[0][0] = accum
        refs[1][0] = jnp.broadcast_to(best, (rows, 8))
        refs[2][0] = jnp.broadcast_to(total, (rows, 8))


def attend(queries, keys, values, swap, part=0, parts=1, state=None):
    groups, rows, width = queries.shape
    heads, tokens, _ = values.shape
    per_head = groups // heads
    block = math.gcd(rows, 768)
    chunk = math.gcd(tokens, 1024)
    scale = 1.0 / math.sqrt(width)
    finish = part == parts - 1
    wide = pl.BlockSpec((1, block, width), lambda g, i: (g, i, 0))
    thin = pl.BlockSpec((1, block, 8), lambda g, i: (g, i, 0))
    thin_shape = jax.ShapeDtypeStruct((groups, rows, 8), jnp.float32)
    state = () if state is None else tuple(state)
    wide_type = jnp.bfloat16 if finish else jnp.float32
    return pl.pallas_call(
        functools.partial(attend_kernel, chunk, scale, bool(state), finish),
        grid=(groups, rows // block),
        in_specs=[
            pl.BlockSpec(memory_space=pltpu.SMEM),
            wide,
            pl.BlockSpec((1, tokens, width), lambda g, i: (g // per_head, part, 0)),
            pl.BlockSpec((1, tokens, width), lambda g, i: (g // per_head, 0, 0)),
        ]
        + ([wide, thin, thin] if state else []),
        out_specs=[wide, thin] if finish else [wide, thin, thin],
        out_shape=[jax.ShapeDtypeStruct((groups, rows, width), wide_type), thin_shape]
        + ([] if finish else [thin_shape]),
        cost_estimate=pl.CostEstimate(
            flops=8 * groups * rows * tokens * width,
            bytes_accessed=4 * groups * rows * width * 2,
            transcendentals=groups * rows * tokens,
        ),
    )(swap.reshape(1), queries, keys, values, *state)


def nodes(count, order, pad):
    half = np.log((count - 1 + pad) / pad)
    e = np.exp(half * np.cos(np.pi * (2 * np.arange(order) + 1) / (2 * order)))
    return ((count - 1 + pad) * e - pad) / (1 + e)


def cardinals(places, count, order, pad):
    half = np.log((count - 1 + pad) / pad)
    at = np.arccos(np.clip(np.log((places + pad) / (count - 1 + pad - places)) / half, -1.0, 1.0))
    own = np.pi * (2 * np.arange(order) + 1) / (2 * order)
    total = np.zeros((places.size, order))
    for k in range(order):
        total += (1.0 if k == 0 else 2.0) / order * np.cos(k * at)[:, None] * np.cos(k * own)[None, :]
    return total


@functools.lru_cache(maxsize=None)
def fields(length, devices):
    parts, order = PARTS, ORDER
    scale = math.sqrt(0.5) / (2 * length)

    def cot(m):
        return 1.0 / np.tan(np.pi * m / (4 * length))

    n_dev = length // devices
    n_part, t_dev = n_dev // parts, n_dev // 2
    t_part = n_part // 2
    n, t = np.arange(n_part), np.arange(t_part)
    sign_n = np.array([1.0, -1.0, -1.0, 1.0])[n % 4]
    sign_t = np.where(t % 2 == 0, 1.0, -1.0)
    near = sign_t[:, None] * sign_n * scale * cot(4 * t[:, None] - 2 * n + 1.0)
    down = cardinals(n, n_part, order, 1.5).T * sign_n
    up = sign_t[:, None] * cardinals(t, t_part, order, 0.75)
    part = np.arange(parts)[:, None]
    source = (part * n_part + nodes(n_part, order, 1.5)).reshape(-1)
    target = (part * t_part + nodes(t_part, order, 0.75)).reshape(-1)
    merge = cardinals(source, n_dev, order, 1.5).T
    own = np.arange(parts * order) // order
    same = own[:, None] == own[None, :]
    local = np.where(same, 0.0, scale * cot(np.where(same, 1.0, 4 * target[:, None] - 2 * source + 1)))
    whole = nodes(n_dev, order, 1.5)
    cross = np.zeros((devices, parts * order, devices, order))
    for r in range(devices):
        for d in range(devices):
            a = 4 * (target + r * t_dev)[:, None]
            b = 2 * (whole + (r - d) % devices * n_dev)
            cross[r, :, d] = scale * cot(a + b + 3)
            if d:
                cross[r, :, d] += scale * cot(a - b + 1)
    return near, down, up, local, merge, cross.reshape(devices, parts * order, devices * order)


def spins(places, width):
    freq = 500000.0 ** (-2.0 * np.arange(width // 2) / width)
    angles = places[:, None] * freq
    cosine, sine = np.cos(angles), np.sin(angles)
    return np.stack(
        [np.concatenate([cosine, cosine], axis=1), np.concatenate([-sine, sine], axis=1)]
    ).astype(np.float32)


def fused_kernel(
    count,
    factor,
    keys_ref,
    values_ref,
    asked_ref,
    near_ref,
    down_ref,
    up_ref,
    local_ref,
    merge_ref,
    cross_hbm,
    coarse_ref,
    fine_ref,
    out_ref,
    cross_ref,
    parts_ref,
    whole_ref,
    others_ref,
    close_ref,
    field_ref,
    k_ref,
    v_ref,
    scores_ref,
    asks_ref,
    sent_ref,
    sent_log_ref,
    got_ref,
    got_log_ref,
    cross_sem,
    field_send,
    field_recv,
    ask_send,
    ask_recv,
    part_send,
    part_recv,
    log_send,
    log_recv,
):
    me = lax.axis_index("ctx")
    heads, width, rows = asked_ref.shape
    order = whole_ref.shape[0]
    n_part = near_ref.shape[1]
    t_part = n_part // 2
    half_columns = keys_ref.shape[1]
    tokens = k_ref.shape[1]

    def copy(src, dst, send, recv, step):
        return pltpu.make_async_remote_copy(
            src_ref=src,
            dst_ref=dst,
            send_sem=send,
            recv_sem=recv,
            device_id={"ctx": lax.rem(me + step, count)},
            device_id_type=MESH,
        )

    fetch = pltpu.make_async_copy(cross_hbm.at[me], cross_ref, cross_sem)
    fetch.start()
    barrier = pltpu.get_barrier_semaphore()
    for step in range(1, count):
        pl.semaphore_signal(
            barrier, inc=1, device_id={"ctx": lax.rem(me + step, count)}, device_id_type=MESH
        )
    pl.semaphore_wait(barrier, count - 1)

    for p in range(PARTS):
        for side, x_ref in enumerate((keys_ref, values_ref)):
            z = jnp.dot(
                down_ref[...], x_ref[p * n_part : (p + 1) * n_part, :], preferred_element_type=jnp.float32
            )
            parts_ref[
                p * order : (p + 1) * order, side * half_columns : (side + 1) * half_columns
            ] = z[:order] + z[order:]
    whole_ref[...] = strict_dot(merge_ref[...], parts_ref[...])
    field_copies = [
        copy(whole_ref, others_ref.at[step - 1], field_send.at[step - 1], field_recv.at[step - 1], step)
        for step in range(1, count)
    ]
    for each in field_copies:
        each.start()
    ask_copies = [
        copy(asked_ref, asks_ref.at[step - 1], ask_send.at[step - 1], ask_recv.at[step - 1], step)
        for step in range(1, count)
    ]
    for each in ask_copies:
        each.start()

    def close(p, carry):
        start = pl.multiple_of(p * n_part, n_part)
        for side, x_ref in enumerate((keys_ref, values_ref)):
            z = jnp.dot(near_ref[...], x_ref[pl.ds(start, n_part), :], preferred_element_type=jnp.float32)
            close_ref[p, :, side * half_columns : (side + 1) * half_columns] = z[:t_part] + z[t_part:]
        return carry

    lax.fori_loop(0, PARTS, close, 0)
    asks_ref[count - 1] = asked_ref[...]
    field_ref[...] = strict_dot(local_ref[...], parts_ref[...])
    fetch.wait()
    for each in field_copies:
        each.wait_recv()
    field_ref[...] += strict_dot(
        cross_ref[...],
        jnp.concatenate([whole_ref[...]] + [others_ref[i] for i in range(count - 1)], axis=0),
    )

    def finish(p, carry):
        f = field_ref[pl.ds(pl.multiple_of(p * order, order), order), :]
        high = f.astype(jnp.bfloat16)
        low = (f - high.astype(jnp.float32)).astype(jnp.bfloat16)
        y = close_ref[p] + jnp.dot(
            up_ref[...], jnp.concatenate([high, low, high], axis=0), preferred_element_type=jnp.float32
        )
        y = y.astype(jnp.bfloat16).astype(jnp.float32)
        begin = pl.multiple_of(p * t_part, t_part)
        place = me * PARTS + p
        cos_p, sin_p = coarse_ref[0, pl.ds(place, 1), :], coarse_ref[1, pl.ds(place, 1), :]
        cosine = cos_p * fine_ref[0] - sin_p * fine_ref[1]
        sine = sin_p * fine_ref[0] + cos_p * fine_ref[1]
        for head in range(heads):
            k = y[:, head * width : (head + 1) * width]
            turned = k * cosine + pltpu.roll(k, width // 2, 1) * sine
            k_ref[head, pl.ds(begin, t_part), :] = turned.astype(jnp.bfloat16)
            v = y[:, half_columns + head * width : half_columns + (head + 1) * width]
            v_ref[head, :, pl.ds(begin, t_part)] = v.T.astype(jnp.bfloat16)
        return carry

    lax.fori_loop(0, PARTS, finish, 0)

    def attend_one(slot, head):
        chunk = 512
        for block in range(rows // BLOCK):
            lanes = slice(block * BLOCK, (block + 1) * BLOCK)
            keep = scores_ref.at[block % 2]
            q = asks_ref[slot, head, :, lanes]
            best = None
            for c in range(0, tokens, chunk):
                s = jnp.dot(k_ref[head, c : c + chunk, :], q, preferred_element_type=jnp.float32)
                keep[c : c + chunk, :] = s
                top = jnp.max(s, axis=0, keepdims=True)
                best = top if best is None else jnp.maximum(best, top)
            total = jnp.zeros((1, BLOCK), jnp.float32)
            accum = jnp.zeros((width, BLOCK), jnp.float32)
            for c in range(0, tokens, chunk):
                e = jnp.exp2((keep[c : c + chunk, :] - best) * factor)
                total += jnp.sum(e, axis=0, keepdims=True)
                accum += jnp.dot(
                    v_ref[head, :, c : c + chunk], e.astype(jnp.bfloat16), preferred_element_type=jnp.float32
                )
            sent_ref[slot, head, :, lanes] = (accum / total).astype(jnp.bfloat16)
            sent_log_ref[slot, head, :, lanes] = jnp.broadcast_to(best * factor + jnp.log2(total), (8, BLOCK))

    def part_copy(slot, head):
        return copy(
            sent_ref.at[slot, head],
            got_ref.at[slot, head],
            part_send.at[slot, head],
            part_recv.at[slot, head],
            count - 1 - slot,
        )

    def log_copy(slot, head):
        return copy(
            sent_log_ref.at[slot, head],
            got_log_ref.at[slot, head],
            log_send.at[slot, head],
            log_recv.at[slot, head],
            count - 1 - slot,
        )

    def serve(i, carry):
        slot, head = i // heads, lax.rem(i, heads)

        @pl.when(jnp.logical_and(head == 0, slot < count - 1))
        def _():
            copy(asked_ref, asks_ref.at[slot], ask_send.at[slot], ask_recv.at[slot], slot + 1).wait_recv()

        attend_one(slot, head)

        @pl.when(slot < count - 1)
        def _():
            part_copy(slot, head).start()
            log_copy(slot, head).start()

        return carry

    lax.fori_loop(0, count * heads, serve, 0)

    for each in field_copies + ask_copies:
        each.wait_send()
    for slot in range(count - 1):
        for head in range(heads):
            part_copy(slot, head).wait()
            log_copy(slot, head).wait()
    for head in range(heads):
        logs = [got_log_ref[i, head, :1, :] for i in range(count - 1)] + [sent_log_ref[count - 1, head, :1, :]]
        best = functools.reduce(jnp.maximum, logs)
        shares = [jnp.exp2(log - best) for log in logs]
        total = functools.reduce(jnp.add, shares)
        parts = [got_ref[i, head] for i in range(count - 1)] + [sent_ref[count - 1, head]]
        mixed = functools.reduce(
            jnp.add, [part.astype(jnp.float32) * (share / total) for part, share in zip(parts, shares)]
        )
        out_ref[head] = mixed.T.astype(out_ref.dtype)


def by_tokens(keys, values, queries, positions, count):
    heads, rows, width = queries.shape
    n_dev, columns = keys.shape
    length = n_dev * count
    near, down, up, local, merge, cross = fields(length, count)

    def tall(matrix):
        return np.concatenate(split_two(matrix), axis=-2)

    up_high, up_low = split_two(up)
    t_part = near.shape[0]
    rotated = rotate_rows(queries.astype(jnp.float32), positions.astype(jnp.float32)).astype(
        jnp.bfloat16
    )
    asked = rotated.swapaxes(1, 2)
    tokens = n_dev // 2
    coarse = spins(np.arange(count * PARTS) * float(t_part), width)
    fine = spins(np.arange(t_part) * 1.0, width)
    vmem = pl.BlockSpec(memory_space=pltpu.VMEM)
    dma = pltpu.SemaphoreType.DMA
    return pl.pallas_call(
        functools.partial(fused_kernel, count, math.log2(math.e) / math.sqrt(width)),
        in_specs=[vmem] * 8 + [pl.BlockSpec(memory_space=pl.ANY)] + [vmem] * 2,
        out_specs=vmem,
        out_shape=jax.ShapeDtypeStruct(queries.shape, jnp.bfloat16),
        scratch_shapes=[
            pltpu.VMEM((2 * PARTS * ORDER, count * ORDER), jnp.bfloat16),
            pltpu.VMEM((PARTS * ORDER, 2 * columns), jnp.float32),
            pltpu.VMEM((ORDER, 2 * columns), jnp.float32),
            pltpu.VMEM((count - 1, ORDER, 2 * columns), jnp.float32),
            pltpu.VMEM((PARTS, t_part, 2 * columns), jnp.float32),
            pltpu.VMEM((PARTS * ORDER, 2 * columns), jnp.float32),
            pltpu.VMEM((heads, tokens, width), jnp.bfloat16),
            pltpu.VMEM((heads, width, tokens), jnp.bfloat16),
            pltpu.VMEM((2, tokens, BLOCK), jnp.float32),
            pltpu.VMEM((count, heads, width, rows), jnp.bfloat16),
            pltpu.VMEM((count, heads, width, rows), jnp.bfloat16),
            pltpu.VMEM((count, heads, 8, rows), jnp.float32),
            pltpu.VMEM((count - 1, heads, width, rows), jnp.bfloat16),
            pltpu.VMEM((count - 1, heads, 8, rows), jnp.float32),
            dma,
            dma((count - 1,)),
            dma((count - 1,)),
            dma((count - 1,)),
            dma((count - 1,)),
            dma((count - 1, heads)),
            dma((count - 1, heads)),
            dma((count - 1, heads)),
            dma((count - 1, heads)),
        ],
        compiler_params=pltpu.CompilerParams(
            collective_id=0, has_side_effects=True, vmem_limit_bytes=60 * 1024 * 1024
        ),
    )(
        keys,
        values,
        asked,
        tall(near),
        tall(down),
        np.concatenate([up_high, up_high, up_low], axis=1),
        tall(local),
        tall(merge),
        tall(cross),
        coarse,
        fine,
    )


def by_columns(keys, values, queries, positions):
    key_parts = lax.all_to_all(keys, "ctx", split_axis=1, concat_axis=0, tiled=True)
    value_parts = lax.all_to_all(values, "ctx", split_axis=1, concat_axis=0, tiled=True)
    heads, rows, width = queries.shape
    per_device = key_parts.shape[1]
    compact = compress(jnp.concatenate([key_parts, value_parts], axis=1))
    rotated = rotate_rows(queries.astype(jnp.float32), positions.astype(jnp.float32)).astype(
        jnp.bfloat16
    )
    whole = lax.all_gather(compact.T, "ctx", axis=0, tiled=True)
    tokens = whole.shape[1]
    shaped = whole.reshape(-1, 2, per_device, tokens)
    key_rows = shaped[:, 0].reshape(heads, width, tokens).swapaxes(1, 2)
    value_rows = shaped[:, 1].reshape(heads, width, tokens).swapaxes(1, 2)
    places = jnp.arange(tokens).astype(jnp.float32)
    ready = rotate_rows(key_rows.astype(jnp.float32), places).astype(jnp.bfloat16)
    return attend(rotated, ready, value_rows, jnp.zeros((), jnp.int32))[0]


def solution(mesh):
    count = mesh.shape["ctx"]

    def on_device(keys, values, queries, positions):
        heads, rows, width = queries.shape
        if count <= 2 * heads and keys.shape[0] % (PARTS * 512) == 0 and rows % BLOCK == 0:
            return by_tokens(keys, values, queries, positions, count)
        return by_columns(keys, values, queries, positions)

    return jax.shard_map(
        on_device,
        mesh=mesh,
        in_specs=(
            P(("user", "ctx"), "heads"),
            P(("user", "ctx"), "heads"),
            P("heads", ("user", "ctx"), None),
            P(("user", "ctx")),
        ),
        out_specs=P("heads", ("user", "ctx"), None),
        check_vma=False,
    )
```

time: 215 us -> 115 us (0.53)
  waiting for transfers between devices: 102 us -> 0 us
  Pallas kernels: 63.9 us -> 109 us
  blocking collectives: 21 us -> 0 us
  starting transfers between devices: 12.2 us -> 0 us
  other arithmetic: 7.81 us -> 2.38 us
  local copies, waits for them, and re-layouts: 7.1 us -> 2.94 us
    all_to_all x2 -> x0, waiting for transfers between devices: 89.2 us -> none  [the longest x1 89.2 us: by_pairs(): lax.all_to_all(jnp.stack(pieces), 'ctx', split_axis=0, concat_axis=0, til...]
    pallas_call x3 -> x1, Pallas kernels: 63.9 us -> 109 us  [by_tokens(): pl.pallas_call(functools.partial(fused_kernel, count, math.log2(math.e) /...]
    all_to_all x1 -> x0, blocking collectives: 21 us -> none  [by_pairs(): lax.all_to_all(jnp.concatenate([part, top, mid, last], axis=1), 'ctx', sp...]
    ppermute x2 -> x0, waiting for transfers between devices: 13 us -> none  [by_pairs(): others = [lax.ppermute(send, 'ctx', pairs) for send in sends]]
    all_to_all x2 -> x0, starting transfers between devices: 10.2 us -> none  [the longest x1 6.48 us: by_pairs(): lax.all_to_all(jnp.stack(pieces), 'ctx', split_axis=0, concat_axis=0, til...]
    another operation x6 -> x1, other arithmetic: 4.12 us -> 0.1 us  [the longest x1 2.26 us: by_pairs(): jnp.stack(pieces)]
    another operation x2 -> x0, local copies, waits for them, and re-layouts: 2.45 us -> none  [the longest x1 2.44 us: by_pairs(): jnp.stack(pieces)]
  transfers between devices with their start and end apart: 4 -> 0, of which waited for: 2 -> 0; matrix products, arithmetic and copies ran while one was open for 2% -> 0% of each run, Pallas kernels for 19% -> 0%
where the time goes in v1:
time: 115 us
  Pallas kernels  109 us (95%)
  local copies, waits for them, and re-layouts  2.94 us (3%)
  other arithmetic  2.38 us (2%)
    pallas_call x1, Pallas kernels, by_tokens(): pl.pallas_call(functools.partial(fused_kernel, count, math.log2(math.e) /...  109 us
    unnamed x2, local copies, waits for them, and re-layouts  2.94 us

profile of v1, /device:TPU:0, one launch (start us, length us, event | category | flops | bytes accessed | tf_op | source)
XLA Modules:
  0.0 114.8 jit_solution(17825490222401047786)
XLA Ops:
  0.0 0.7 convert_element_type.15
  0.7 0.8 multiply_cosine_fusion
  1.5 1.2 %copy.13 = bf16[2,768,128]{1,2,0:T(8,128)(2,1)S(1)} copy(bf16[2,768,128]{2,1,0:T(8,128)(2,1)} %param.14) | data formatting | bytes 786432 | tf_op args[2]
  2.6 0.1 convert_element_type.14
  2.7 0.1 subtract_convert_fusion
  2.8 0.8 maximum_bitcast_fusion.asked_ref
  3.6 109.5 %shard_map.118 = bf16[2,768,128]{2,1,0:T(8,128)(2,1)} custom-call(bf16[4096,256]{1,0:T(8,128)(2,1)} %keys_ref.1, bf16[4096,256]{1,0:T(8,128)(2,1)} %values_ref.1, bf16[2,128,768]{2,1,0:T(8,128)(2,1)} %maximum_bitcast_fusion.asked_ref, bf16[1024,1024]{1,0:T(8,128)(2,1)} %constant.18.clone.near_ref, bf16[128,1024]{1,0:T(8,128)(2,1)} %constant.19.clone.down_ref, ...), custom_call_target="tpu_custom_call" | custom-call | tf_op jit(solution)/shard_map/pallas_call | solution.py:467
  113.1 1.8 %copy.15 = bf16[2,768,128]{2,1,0:T(8,128)(2,1)} copy(bf16[2,768,128]{2,1,0:T(8,128)(2,1)} %shard_map.118) | data formatting | bytes 786432
  (1 shorter events, 0.0 us)

commit v2 on v1

--- a/solution.py
+++ b/solution.py
@@ -12,6 +12,7 @@
 OUTER = 128
 PARTS = 4
 ORDER = 64
+FAR = 16
 BLOCK = 256
 MESH = pl.DeviceIdType.MESH
 
@@ -213,20 +214,32 @@
     part = np.arange(parts)[:, None]
     source = (part * n_part + nodes(n_part, order, 1.5)).reshape(-1)
     target = (part * t_part + nodes(t_part, order, 0.75)).reshape(-1)
-    merge = cardinals(source, n_dev, order, 1.5).T
+    bend = np.pi * (2 * np.arange(FAR) + 1) / (2 * FAR)
+    spot = np.arccos(np.clip(2.0 * source / (n_dev - 1) - 1.0, -1.0, 1.0))
+    plain = sum(
+        (1.0 if k == 0 else 2.0) / FAR * np.cos(k * bend)[:, None] * np.cos(k * spot)[None, :]
+        for k in range(FAR)
+    )
+    merge = np.concatenate([cardinals(source, n_dev, order, 1.5).T, plain])
     own = np.arange(parts * order) // order
     same = own[:, None] == own[None, :]
     local = np.where(same, 0.0, scale * cot(np.where(same, 1.0, 4 * target[:, None] - 2 * source + 1)))
     whole = nodes(n_dev, order, 1.5)
-    cross = np.zeros((devices, parts * order, devices, order))
+    sparse = (np.cos(bend) + 1.0) * (n_dev - 1) / 2
+    cross = np.zeros((devices, parts * order, 3 * order + devices * FAR))
     for r in range(devices):
-        for d in range(devices):
-            a = 4 * (target + r * t_dev)[:, None]
-            b = 2 * (whole + (r - d) % devices * n_dev)
-            cross[r, :, d] = scale * cot(a + b + 3)
-            if d:
-                cross[r, :, d] += scale * cot(a - b + 1)
-    return near, down, up, local, merge, cross.reshape(devices, parts * order, devices * order)
+        a = 4 * (target + r * t_dev)[:, None]
+        for s in range(devices):
+            b = 2 * ((sparse if abs(r - s) > 1 else whole) + s * n_dev)
+            block = scale * cot(a + b + 3)
+            if r != s:
+                block = block + scale * cot(a - b + 1)
+            if abs(r - s) > 1:
+                start = 3 * order + s * FAR
+            else:
+                start = {0: 0, 1: order, -1: 2 * order}[r - s]
+            cross[r, :, start : start + block.shape[1]] = block
+    return near, down, up, local, merge, cross
 
 
 def spins(places, width):
@@ -263,46 +276,82 @@
     v_ref,
     scores_ref,
     asks_ref,
-    sent_ref,
-    sent_log_ref,
-    got_ref,
-    got_log_ref,
+    own_ref,
+    own_log_ref,
+    half_ref,
+    half_log_ref,
+    merged_ref,
+    merged_log_ref,
+    over_ref,
+    over_log_ref,
+    mate_ref,
+    mate_log_ref,
     cross_sem,
     field_send,
     field_recv,
     ask_send,
     ask_recv,
-    part_send,
-    part_recv,
-    log_send,
-    log_recv,
+    half_send,
+    half_recv,
+    over_send,
+    over_recv,
+    mate_send,
+    mate_recv,
 ):
     me = lax.axis_index("ctx")
     heads, width, rows = asked_ref.shape
-    order = whole_ref.shape[0]
+    order = ORDER
     n_part = near_ref.shape[1]
     t_part = n_part // 2
     half_columns = keys_ref.shape[1]
     tokens = k_ref.shape[1]
-
-    def copy(src, dst, send, recv, step):
+    mate = me + 1 - 2 * lax.rem(me, 2)
+    mine = lax.rem(me, heads)
+
+    def copy(src, dst, send, recv, other):
         return pltpu.make_async_remote_copy(
             src_ref=src,
             dst_ref=dst,
             send_sem=send,
             recv_sem=recv,
-            device_id={"ctx": lax.rem(me + step, count)},
+            device_id={"ctx": other},
             device_id_type=MESH,
         )
 
     fetch = pltpu.make_async_copy(cross_hbm.at[me], cross_ref, cross_sem)
     fetch.start()
+    others_ref[...] = jnp.zeros_like(others_ref)
+    asks_ref[me] = asked_ref[...]
     barrier = pltpu.get_barrier_semaphore()
     for step in range(1, count):
         pl.semaphore_signal(
             barrier, inc=1, device_id={"ctx": lax.rem(me + step, count)}, device_id_type=MESH
         )
     pl.semaphore_wait(barrier, count - 1)
+
+    has_left, has_right = me > 0, me < count - 1
+
+    def ask_copy(source, side):
+        return copy(
+            asks_ref.at[source],
+            asks_ref.at[source],
+            ask_send.at[source, side],
+            ask_recv.at[source],
+            me + 2 * side - 1,
+        )
+
+    def first_copy(side):
+        return copy(
+            asked_ref, asks_ref.at[me], ask_send.at[me, side], ask_recv.at[me], me + 2 * side - 1
+        )
+
+    @pl.when(has_left)
+    def _():
+        first_copy(0).start()
+
+    @pl.when(has_right)
+    def _():
+        first_copy(1).start()
 
     for p in range(PARTS):
         for side, x_ref in enumerate((keys_ref, values_ref)):
@@ -313,18 +362,61 @@
                 p * order : (p + 1) * order, side * half_columns : (side + 1) * half_columns
             ] = z[:order] + z[order:]
     whole_ref[...] = strict_dot(merge_ref[...], parts_ref[...])
-    field_copies = [
-        copy(whole_ref, others_ref.at[step - 1], field_send.at[step - 1], field_recv.at[step - 1], step)
-        for step in range(1, count)
-    ]
-    for each in field_copies:
-        each.start()
-    ask_copies = [
-        copy(asked_ref, asks_ref.at[step - 1], ask_send.at[step - 1], ask_recv.at[step - 1], step)
-        for step in range(1, count)
-    ]
-    for each in ask_copies:
-        each.start()
+    others_ref[:order] = whole_ref[:order]
+
+    def near_copy(side):
+        start = order * (2 - side)
+        return copy(
+            whole_ref.at[pl.ds(0, order)],
+            others_ref.at[pl.ds(start, order)],
+            field_send.at[me + 2 * side - 1],
+            field_recv.at[me],
+            me + 2 * side - 1,
+        )
+
+    def far_copy(other):
+        return copy(
+            whole_ref.at[pl.ds(order, FAR)],
+            others_ref.at[pl.ds(pl.multiple_of(3 * order + me * FAR, FAR), FAR)],
+            field_send.at[other],
+            field_recv.at[me],
+            other,
+        )
+
+    def near_wait(side):
+        start = order * (1 + side)
+        source = me + 2 * side - 1
+        copy(
+            whole_ref.at[pl.ds(0, order)],
+            others_ref.at[pl.ds(start, order)],
+            field_send.at[source],
+            field_recv.at[source],
+            source,
+        ).wait_recv()
+
+    def far_wait(source):
+        copy(
+            whole_ref.at[pl.ds(order, FAR)],
+            others_ref.at[pl.ds(3 * order + source * FAR, FAR)],
+            field_send.at[source],
+            field_recv.at[source],
+            source,
+        ).wait_recv()
+
+    def far_from(other):
+        return jnp.logical_or(other - me > 1, me - other > 1)
+
+    for side, there in enumerate((has_left, has_right)):
+
+        @pl.when(there)
+        def _():
+            near_copy(side).start()
+
+    for other in range(count):
+
+        @pl.when(far_from(other))
+        def _():
+            far_copy(other).start()
 
     def close(p, carry):
         start = pl.multiple_of(p * n_part, n_part)
@@ -334,15 +426,37 @@
         return carry
 
     lax.fori_loop(0, PARTS, close, 0)
-    asks_ref[count - 1] = asked_ref[...]
     field_ref[...] = strict_dot(local_ref[...], parts_ref[...])
+
+    @pl.when(has_left)
+    def _():
+        ask_copy(me - 1, 1).wait_recv()
+
+    @pl.when(has_right)
+    def _():
+        ask_copy(me + 1, 0).wait_recv()
+
+    inside = jnp.logical_and(has_left, has_right)
+
+    @pl.when(inside)
+    def _():
+        ask_copy(me - 1, 1).start()
+        ask_copy(me + 1, 0).start()
+
     fetch.wait()
-    for each in field_copies:
-        each.wait_recv()
-    field_ref[...] += strict_dot(
-        cross_ref[...],
-        jnp.concatenate([whole_ref[...]] + [others_ref[i] for i in range(count - 1)], axis=0),
-    )
+    for side, there in enumerate((has_left, has_right)):
+
+        @pl.when(there)
+        def _():
+            near_wait(side)
+
+    for other in range(count):
+
+        @pl.when(far_from(other))
+        def _():
+            far_wait(other)
+
+    field_ref[...] += strict_dot(cross_ref[...], others_ref[...])
 
     def finish(p, carry):
         f = field_ref[pl.ds(pl.multiple_of(p * order, order), order), :]
@@ -367,12 +481,23 @@
 
     lax.fori_loop(0, PARTS, finish, 0)
 
-    def attend_one(slot, head):
+    lower = me < count // 2
+    far_end = jnp.where(lower, count - 1, 0)
+    near_over = jnp.where(lower, count // 2, count // 2 - 1)
+    out_side = jnp.where(lower, 0, 1)
+
+    @pl.when(inside)
+    def _():
+        handed = ask_copy(far_end, out_side)
+        handed.wait_recv()
+        handed.start()
+
+    def attend_one(slot, source, head):
         chunk = 512
         for block in range(rows // BLOCK):
             lanes = slice(block * BLOCK, (block + 1) * BLOCK)
             keep = scores_ref.at[block % 2]
-            q = asks_ref[slot, head, :, lanes]
+            q = asks_ref[source, head, :, lanes]
             best = None
             for c in range(0, tokens, chunk):
                 s = jnp.dot(k_ref[head, c : c + chunk, :], q, preferred_element_type=jnp.float32)
@@ -387,61 +512,152 @@
                 accum += jnp.dot(
                     v_ref[head, :, c : c + chunk], e.astype(jnp.bfloat16), preferred_element_type=jnp.float32
                 )
-            sent_ref[slot, head, :, lanes] = (accum / total).astype(jnp.bfloat16)
-            sent_log_ref[slot, head, :, lanes] = jnp.broadcast_to(best * factor + jnp.log2(total), (8, BLOCK))
-
-    def part_copy(slot, head):
-        return copy(
-            sent_ref.at[slot, head],
-            got_ref.at[slot, head],
-            part_send.at[slot, head],
-            part_recv.at[slot, head],
-            count - 1 - slot,
-        )
-
-    def log_copy(slot, head):
-        return copy(
-            sent_log_ref.at[slot, head],
-            got_log_ref.at[slot, head],
-            log_send.at[slot, head],
-            log_recv.at[slot, head],
-            count - 1 - slot,
-        )
-
-    def serve(i, carry):
-        slot, head = i // heads, lax.rem(i, heads)
-
-        @pl.when(jnp.logical_and(head == 0, slot < count - 1))
-        def _():
-            copy(asked_ref, asks_ref.at[slot], ask_send.at[slot], ask_recv.at[slot], slot + 1).wait_recv()
-
-        attend_one(slot, head)
-
-        @pl.when(slot < count - 1)
-        def _():
-            part_copy(slot, head).start()
-            log_copy(slot, head).start()
-
-        return carry
-
-    lax.fori_loop(0, count * heads, serve, 0)
-
-    for each in field_copies + ask_copies:
-        each.wait_send()
-    for slot in range(count - 1):
-        for head in range(heads):
-            part_copy(slot, head).wait()
-            log_copy(slot, head).wait()
-    for head in range(heads):
-        logs = [got_log_ref[i, head, :1, :] for i in range(count - 1)] + [sent_log_ref[count - 1, head, :1, :]]
+            own_ref[slot, head, :, lanes] = (accum / total).astype(jnp.bfloat16)
+            own_log_ref[slot, head, :, lanes] = best * factor + jnp.log2(total)
+
+    def both(src, src_log, dst, dst_log, send, recv, other):
+        return (
+            copy(src, dst, send.at[0], recv.at[0], other),
+            copy(src_log, dst_log, send.at[1], recv.at[1], other),
+        )
+
+    def half_copy(j):
+        return both(
+            own_ref.at[j + 1, 1 - mine],
+            own_log_ref.at[j + 1, 1 - mine],
+            half_ref.at[j],
+            half_log_ref.at[j],
+            half_send.at[j],
+            half_recv.at[j],
+            mate,
+        )
+
+    def over_copy(j):
+        return both(
+            merged_ref.at[j],
+            merged_log_ref.at[j],
+            over_ref.at[mine],
+            over_log_ref.at[mine],
+            over_send.at[j],
+            over_recv.at[mine],
+            near_over if j == 0 else far_end,
+        )
+
+    def mate_copy(head):
+        return both(
+            own_ref.at[3, head],
+            own_log_ref.at[3, head],
+            mate_ref.at[head],
+            mate_log_ref.at[head],
+            mate_send.at[head],
+            mate_recv.at[head],
+            mate,
+        )
+
+    def blend(parts, logs):
         best = functools.reduce(jnp.maximum, logs)
         shares = [jnp.exp2(log - best) for log in logs]
         total = functools.reduce(jnp.add, shares)
-        parts = [got_ref[i, head] for i in range(count - 1)] + [sent_ref[count - 1, head]]
         mixed = functools.reduce(
             jnp.add, [part.astype(jnp.float32) * (share / total) for part, share in zip(parts, shares)]
         )
+        return mixed, best + jnp.log2(total)
+
+    def merge_half(j):
+        for each in half_copy(j):
+            each.wait_recv()
+        mixed, log = blend(
+            [own_ref[j + 1, mine], half_ref[j]], [own_log_ref[j + 1, mine], half_log_ref[j]]
+        )
+        merged_ref[j] = mixed.astype(jnp.bfloat16)
+        merged_log_ref[j] = log
+        for each in over_copy(j):
+            each.start()
+
+    def serve(u, carry):
+        slot = u // heads
+        second = lax.rem(u, heads)
+        head = jnp.where(second == 0, 1 - mine, mine)
+        source = jnp.where(
+            slot == 0, me, jnp.where(slot == 1, near_over, jnp.where(slot == 2, far_end, mate))
+        )
+
+        @pl.when(
+            jnp.logical_and(
+                jnp.logical_and(second == 0, jnp.logical_not(inside)),
+                jnp.logical_or(slot == 1, slot == 2),
+            )
+        )
+        def _():
+            ask_copy(source, 1 - out_side).wait_recv()
+
+        attend_one(slot, source, head)
+        for j in range(2):
+
+            @pl.when(u == (j + 1) * heads)
+            def _():
+                for each in half_copy(j):
+                    each.start()
+
+            @pl.when(u == (j + 2) * heads)
+            def _():
+                merge_half(j)
+
+        @pl.when(slot == 3)
+        def _():
+            for each in mate_copy(head):
+                each.start()
+
+        return carry
+
+    lax.fori_loop(0, 4 * heads, serve, 0)
+
+    for head in range(heads):
+        for each in both(
+            merged_ref.at[0],
+            merged_log_ref.at[0],
+            over_ref.at[head],
+            over_log_ref.at[head],
+            over_send.at[0],
+            over_recv.at[head],
+            near_over,
+        ):
+            each.wait_recv()
+    for head in range(heads):
+        for each in mate_copy(head):
+            each.wait_recv()
+    for head in range(heads):
+        mixed, _ = blend(
+            [own_ref[0, head], over_ref[head], mate_ref[head]],
+            [own_log_ref[0, head], over_log_ref[head], mate_log_ref[head]],
+        )
         out_ref[head] = mixed.T.astype(out_ref.dtype)
+
+    for side, there in enumerate((has_left, has_right)):
+
+        @pl.when(there)
+        def _():
+            first_copy(side).wait_send()
+            near_copy(side).wait_send()
+
+    for other in range(count):
+
+        @pl.when(far_from(other))
+        def _():
+            far_copy(other).wait_send()
+
+    @pl.when(inside)
+    def _():
+        ask_copy(me - 1, 1).wait_send()
+        ask_copy(me + 1, 0).wait_send()
+        ask_copy(far_end, out_side).wait_send()
+
+    for j in range(2):
+        for each in half_copy(j) + over_copy(j):
+            each.wait_send()
+    for head in range(heads):
+        for each in mate_copy(head):
+            each.wait_send()
 
 
 def by_tokens(keys, values, queries, positions, count):
@@ -470,29 +686,37 @@
         out_specs=vmem,
         out_shape=jax.ShapeDtypeStruct(queries.shape, jnp.bfloat16),
         scratch_shapes=[
-            pltpu.VMEM((2 * PARTS * ORDER, count * ORDER), jnp.bfloat16),
+            pltpu.VMEM((2 * cross.shape[1], cross.shape[2]), jnp.bfloat16),
             pltpu.VMEM((PARTS * ORDER, 2 * columns), jnp.float32),
-            pltpu.VMEM((ORDER, 2 * columns), jnp.float32),
-            pltpu.VMEM((count - 1, ORDER, 2 * columns), jnp.float32),
+            pltpu.VMEM((ORDER + FAR, 2 * columns), jnp.float32),
+            pltpu.VMEM((cross.shape[2], 2 * columns), jnp.float32),
             pltpu.VMEM((PARTS, t_part, 2 * columns), jnp.float32),
             pltpu.VMEM((PARTS * ORDER, 2 * columns), jnp.float32),
             pltpu.VMEM((heads, tokens, width), jnp.bfloat16),
             pltpu.VMEM((heads, width, tokens), jnp.bfloat16),
             pltpu.VMEM((2, tokens, BLOCK), jnp.float32),
             pltpu.VMEM((count, heads, width, rows), jnp.bfloat16),
-            pltpu.VMEM((count, heads, width, rows), jnp.bfloat16),
-            pltpu.VMEM((count, heads, 8, rows), jnp.float32),
-            pltpu.VMEM((count - 1, heads, width, rows), jnp.bfloat16),
-            pltpu.VMEM((count - 1, heads, 8, rows), jnp.float32),
+            pltpu.VMEM((4, heads, width, rows), jnp.bfloat16),
+            pltpu.VMEM((4, heads, 1, rows), jnp.float32),
+            pltpu.VMEM((2, width, rows), jnp.bfloat16),
+            pltpu.VMEM((2, 1, rows), jnp.float32),
+            pltpu.VMEM((2, width, rows), jnp.bfloat16),
+            pltpu.VMEM((2, 1, rows), jnp.float32),
+            pltpu.VMEM((heads, width, rows), jnp.bfloat16),
+            pltpu.VMEM((heads, 1, rows), jnp.float32),
+            pltpu.VMEM((heads, width, rows), jnp.bfloat16),
+            pltpu.VMEM((heads, 1, rows), jnp.float32),
             dma,
-            dma((count - 1,)),
-            dma((count - 1,)),
-            dma((count - 1,)),
-            dma((count - 1,)),
-            dma((count - 1, heads)),
-            dma((count - 1, heads)),
-            dma((count - 1, heads)),
-            dma((count - 1, heads)),
+            dma((count,)),
+            dma((count,)),
+            dma((count, 2)),
+            dma((count,)),
+            dma((2, 2)),
+            dma((2, 2)),
+            dma((2, 2)),
+            dma((heads, 2)),
+            dma((heads, 2)),
+            dma((heads, 2)),
         ],
         compiler_params=pltpu.CompilerParams(
             collective_id=0, has_side_effects=True, vmem_limit_bytes=60 * 1024 * 1024
@@ -536,7 +760,7 @@
 
     def on_device(keys, values, queries, positions):
         heads, rows, width = queries.shape
-        if count <= 2 * heads and keys.shape[0] % (PARTS * 512) == 0 and rows % BLOCK == 0:
+        if count == 4 and heads == 2 and keys.shape[0] % (PARTS * 512) == 0 and rows % BLOCK == 0:
             return by_tokens(keys, values, queries, positions, count)
         return by_columns(keys, values, queries, positions)
 

time: 115 us -> 77.2 us (0.67)
  Pallas kernels: 109 us -> 71.7 us
    pallas_call x1, Pallas kernels: 109 us -> 71.7 us  [by_tokens(): pl.pallas_call(functools.partial(fused_kernel, count, math.log2(math.e) /...]
where the time goes in v2:
time: 77.2 us; the launch traced here: 77 us
  Pallas kernels  71.7 us (93%)
  local copies, waits for them, and re-layouts  2.94 us (4%)
  other arithmetic  2.38 us (3%)
    pallas_call x1, Pallas kernels, by_tokens(): pl.pallas_call(functools.partial(fused_kernel, count, math.log2(math.e) /...  71.7 us
    unnamed x2, local copies, waits for them, and re-layouts  2.94 us

profile of v2, /device:TPU:0, one launch (start us, length us, event | category | flops | bytes accessed | tf_op | source)
XLA Modules:
  0.0 77.0 jit_solution(1427651221118872792)
XLA Ops:
  0.0 0.7 convert_element_type.15
  0.7 0.8 multiply_cosine_fusion
  1.5 1.2 %copy.13 = bf16[2,768,128]{1,2,0:T(8,128)(2,1)S(1)} copy(bf16[2,768,128]{2,1,0:T(8,128)(2,1)} %param.14) | data formatting | bytes 786432 | tf_op args[2]
  2.6 0.1 convert_element_type.14
  2.7 0.1 subtract_convert_fusion
  2.8 0.8 %maximum_bitcast_fusion.asked_ref = bf16[2,128,768]{2,1,0:T(8,128)(2,1)} fusion(bf16[2,768,64]{1,2,0:T(8,128)(2,1)S(1)} %get-tuple-element.6, bf16[2,768,64]{1,2,0:T(8,128)(2,1)S(1)} %get-tuple-element.5), kind=kLoop, calls=%fused_computation | loop fusion | flops 786432 | bytes 786432 | tf_op jit(solution)/shard_map/transpose | solution.py:677
  3.6 71.7 %shard_map.118 = bf16[2,768,128]{2,1,0:T(8,128)(2,1)} custom-call(bf16[4096,256]{1,0:T(8,128)(2,1)} %keys_ref.1, bf16[4096,256]{1,0:T(8,128)(2,1)} %values_ref.1, bf16[2,128,768]{2,1,0:T(8,128)(2,1)} %maximum_bitcast_fusion.asked_ref, bf16[1024,1024]{1,0:T(8,128)(2,1)} %constant.18.clone.near_ref, bf16[128,1024]{1,0:T(8,128)(2,1)} %constant.19.clone.down_ref, ...), custom_call_target="tpu_custom_call" | custom-call | tf_op jit(solution)/shard_map/pallas_call | solution.py:683
  75.3 1.8 %copy.15 = bf16[2,768,128]{2,1,0:T(8,128)(2,1)} copy(bf16[2,768,128]{2,1,0:T(8,128)(2,1)} %shard_map.118) | data formatting | bytes 786432
  (1 shorter events, 0.0 us)

commit v3 on v2

--- a/solution.py
+++ b/solution.py
@@ -254,19 +254,35 @@
 def fused_kernel(
     count,
     factor,
+    keys_hbm,
+    values_hbm,
+    queries_hbm,
+    places_hbm,
+    high_hbm,
+    low_hbm,
+    near_hbm,
+    down_hbm,
+    up_hbm,
+    local_hbm,
+    merge_hbm,
+    cross_hbm,
+    coarse_hbm,
+    fine_hbm,
+    out_ref,
     keys_ref,
     values_ref,
-    asked_ref,
+    queries_ref,
+    places_ref,
+    high_ref,
+    low_ref,
     near_ref,
     down_ref,
     up_ref,
     local_ref,
     merge_ref,
-    cross_hbm,
+    cross_ref,
     coarse_ref,
     fine_ref,
-    out_ref,
-    cross_ref,
     parts_ref,
     whole_ref,
     others_ref,
@@ -274,7 +290,10 @@
     field_ref,
     k_ref,
     v_ref,
-    scores_ref,
+    even_ref,
+    odd_ref,
+    even_top_ref,
+    odd_top_ref,
     asks_ref,
     own_ref,
     own_log_ref,
@@ -284,9 +303,12 @@
     merged_log_ref,
     over_ref,
     over_log_ref,
-    mate_ref,
-    mate_log_ref,
-    cross_sem,
+    ready_ref,
+    ready_log_ref,
+    last_ref,
+    last_log_ref,
+    load_sem,
+    token_sem,
     field_send,
     field_recv,
     ask_send,
@@ -295,18 +317,24 @@
     half_recv,
     over_send,
     over_recv,
-    mate_send,
-    mate_recv,
+    last_send,
+    last_recv,
 ):
     me = lax.axis_index("ctx")
-    heads, width, rows = asked_ref.shape
+    heads, rows, width = queries_ref.shape
     order = ORDER
+    blocks = rows // BLOCK
     n_part = near_ref.shape[1]
     t_part = n_part // 2
     half_columns = keys_ref.shape[1]
     tokens = k_ref.shape[1]
+    has_left, has_right = me > 0, me < count - 1
+    inside = jnp.logical_and(has_left, has_right)
+    lower = me < count // 2
     mate = me + 1 - 2 * lax.rem(me, 2)
-    mine = lax.rem(me, heads)
+    far_end = jnp.where(lower, count - 1, 0)
+    near_over = jnp.where(lower, count // 2, count // 2 - 1)
+    outward = jnp.where(lower, 0, 1)
 
     def copy(src, dst, send, recv, other):
         return pltpu.make_async_remote_copy(
@@ -318,43 +346,91 @@
             device_id_type=MESH,
         )
 
-    fetch = pltpu.make_async_copy(cross_hbm.at[me], cross_ref, cross_sem)
-    fetch.start()
     others_ref[...] = jnp.zeros_like(others_ref)
-    asks_ref[me] = asked_ref[...]
     barrier = pltpu.get_barrier_semaphore()
     for step in range(1, count):
         pl.semaphore_signal(
             barrier, inc=1, device_id={"ctx": lax.rem(me + step, count)}, device_id_type=MESH
         )
+    pairs = (
+        (places_hbm, places_ref),
+        (queries_hbm, queries_ref),
+        (high_hbm, high_ref),
+        (low_hbm, low_ref),
+        (down_hbm, down_ref),
+        (merge_hbm, merge_ref),
+        (near_hbm, near_ref),
+        (local_hbm, local_ref),
+        (cross_hbm.at[me], cross_ref),
+        (up_hbm, up_ref),
+        (coarse_hbm, coarse_ref),
+        (fine_hbm, fine_ref),
+    )
+    loads = [pltpu.make_async_copy(src, dst, load_sem.at[i]) for i, (src, dst) in enumerate(pairs)]
+    sides = ((keys_hbm, keys_ref), (values_hbm, values_ref))
+    token_loads = [
+        [
+            pltpu.make_async_copy(
+                src.at[pl.ds(p * n_part, n_part)], dst.at[pl.ds(p * n_part, n_part)], token_sem.at[p, side]
+            )
+            for side, (src, dst) in enumerate(sides)
+        ]
+        for p in range(PARTS)
+    ]
+    for each in loads[:6]:
+        each.start()
+    for p in range(PARTS):
+        for each in token_loads[p]:
+            each.start()
+    for each in loads[6:]:
+        each.start()
+    for each in loads[:4]:
+        each.wait()
+
+    split = low_ref.shape[0] // 2
+    for i in range(rows // split):
+        here = slice(i * split, (i + 1) * split)
+        place = jnp.broadcast_to(places_ref[:, here].astype(jnp.float32), (split, split)).T.astype(jnp.int32)
+        spun = []
+        for value, table_ref in ((place // split, high_ref), (lax.rem(place, split), low_ref)):
+            size = table_ref.shape[0] // 2
+            value = value if size == split else value[:, :1]
+            picked = value == lax.broadcasted_iota(jnp.int32, (split, size), 1)
+            picked = jnp.where(picked, 1.0, 0.0).astype(jnp.bfloat16)
+            got = jnp.dot(
+                jnp.concatenate([picked, picked], axis=1), table_ref[...], preferred_element_type=jnp.float32
+            )
+            spun.append((got[:, :width], got[:, width:]))
+        (cos_a, sin_a), (cos_b, sin_b) = spun
+        cosine, sine = cos_a * cos_b - sin_a * sin_b, sin_a * cos_b + cos_a * sin_b
+        for head in range(heads):
+            x = queries_ref[head, here, :].astype(jnp.float32)
+            asks_ref[me, head, here, :] = (x * cosine + pltpu.roll(x, width // 2, 1) * sine).astype(jnp.bfloat16)
+
+    def ask_copy(source, head, side):
+        return copy(
+            asks_ref.at[source, head],
+            asks_ref.at[source, head],
+            ask_send.at[source, head, side],
+            ask_recv.at[source, head],
+            me + 2 * side - 1,
+        )
+
+    def for_sides(action):
+        for side, there in enumerate((has_left, has_right)):
+
+            @pl.when(there)
+            def _():
+                action(side)
+
     pl.semaphore_wait(barrier, count - 1)
-
-    has_left, has_right = me > 0, me < count - 1
-
-    def ask_copy(source, side):
-        return copy(
-            asks_ref.at[source],
-            asks_ref.at[source],
-            ask_send.at[source, side],
-            ask_recv.at[source],
-            me + 2 * side - 1,
-        )
-
-    def first_copy(side):
-        return copy(
-            asked_ref, asks_ref.at[me], ask_send.at[me, side], ask_recv.at[me], me + 2 * side - 1
-        )
-
-    @pl.when(has_left)
-    def _():
-        first_copy(0).start()
-
-    @pl.when(has_right)
-    def _():
-        first_copy(1).start()
-
+    for_sides(lambda side: ask_copy(me, 0, side).start())
+
+    for each in loads[4:6]:
+        each.wait()
     for p in range(PARTS):
-        for side, x_ref in enumerate((keys_ref, values_ref)):
+        for side, (_, x_ref) in enumerate(sides):
+            token_loads[p][side].wait()
             z = jnp.dot(
                 down_ref[...], x_ref[p * n_part : (p + 1) * n_part, :], preferred_element_type=jnp.float32
             )
@@ -366,12 +442,13 @@
 
     def near_copy(side):
         start = order * (2 - side)
+        other = me + 2 * side - 1
         return copy(
             whole_ref.at[pl.ds(0, order)],
             others_ref.at[pl.ds(start, order)],
-            field_send.at[me + 2 * side - 1],
+            field_send.at[other],
             field_recv.at[me],
-            me + 2 * side - 1,
+            other,
         )
 
     def far_copy(other):
@@ -384,11 +461,10 @@
         )
 
     def near_wait(side):
-        start = order * (1 + side)
         source = me + 2 * side - 1
         copy(
             whole_ref.at[pl.ds(0, order)],
-            others_ref.at[pl.ds(start, order)],
+            others_ref.at[pl.ds(order * (1 + side), order)],
             field_send.at[source],
             field_recv.at[source],
             source,
@@ -403,59 +479,47 @@
             source,
         ).wait_recv()
 
-    def far_from(other):
-        return jnp.logical_or(other - me > 1, me - other > 1)
-
-    for side, there in enumerate((has_left, has_right)):
-
-        @pl.when(there)
-        def _():
-            near_copy(side).start()
-
-    for other in range(count):
-
-        @pl.when(far_from(other))
-        def _():
-            far_copy(other).start()
+    def for_far(action):
+        for other in range(count):
+
+            @pl.when(jnp.logical_or(other - me > 1, me - other > 1))
+            def _():
+                action(other)
+
+    for_sides(lambda side: near_copy(side).start())
+    for_far(lambda other: far_copy(other).start())
+    for_sides(lambda side: ask_copy(me, 1, side).start())
+
+    loads[6].wait()
 
     def close(p, carry):
         start = pl.multiple_of(p * n_part, n_part)
-        for side, x_ref in enumerate((keys_ref, values_ref)):
+        for side, (_, x_ref) in enumerate(sides):
             z = jnp.dot(near_ref[...], x_ref[pl.ds(start, n_part), :], preferred_element_type=jnp.float32)
             close_ref[p, :, side * half_columns : (side + 1) * half_columns] = z[:t_part] + z[t_part:]
         return carry
 
     lax.fori_loop(0, PARTS, close, 0)
+    for each in loads[7:]:
+        each.wait()
     field_ref[...] = strict_dot(local_ref[...], parts_ref[...])
 
-    @pl.when(has_left)
-    def _():
-        ask_copy(me - 1, 1).wait_recv()
-
-    @pl.when(has_right)
-    def _():
-        ask_copy(me + 1, 0).wait_recv()
-
-    inside = jnp.logical_and(has_left, has_right)
-
-    @pl.when(inside)
-    def _():
-        ask_copy(me - 1, 1).start()
-        ask_copy(me + 1, 0).start()
-
-    fetch.wait()
-    for side, there in enumerate((has_left, has_right)):
-
-        @pl.when(there)
+    def hand_on(head):
+        for_sides(lambda side: ask_copy(me + 2 * side - 1, head, 1 - side).wait_recv())
+
+        @pl.when(inside)
         def _():
-            near_wait(side)
-
-    for other in range(count):
-
-        @pl.when(far_from(other))
-        def _():
-            far_wait(other)
-
+            ask_copy(me - 1, head, 1).start()
+            ask_copy(me + 1, head, 0).start()
+
+    def hand_far(head):
+        handed = ask_copy(far_end, head, outward)
+        handed.wait_recv()
+        handed.start()
+
+    hand_on(0)
+    for_sides(near_wait)
+    for_far(far_wait)
     field_ref[...] += strict_dot(cross_ref[...], others_ref[...])
 
     def finish(p, carry):
@@ -481,39 +545,47 @@
 
     lax.fori_loop(0, PARTS, finish, 0)
 
-    lower = me < count // 2
-    far_end = jnp.where(lower, count - 1, 0)
-    near_over = jnp.where(lower, count // 2, count // 2 - 1)
-    out_side = jnp.where(lower, 0, 1)
-
-    @pl.when(inside)
-    def _():
-        handed = ask_copy(far_end, out_side)
-        handed.wait_recv()
-        handed.start()
-
-    def attend_one(slot, source, head):
-        chunk = 512
-        for block in range(rows // BLOCK):
-            lanes = slice(block * BLOCK, (block + 1) * BLOCK)
-            keep = scores_ref.at[block % 2]
-            q = asks_ref[source, head, :, lanes]
-            best = None
-            for c in range(0, tokens, chunk):
-                s = jnp.dot(k_ref[head, c : c + chunk, :], q, preferred_element_type=jnp.float32)
-                keep[c : c + chunk, :] = s
-                top = jnp.max(s, axis=0, keepdims=True)
-                best = top if best is None else jnp.maximum(best, top)
-            total = jnp.zeros((1, BLOCK), jnp.float32)
-            accum = jnp.zeros((width, BLOCK), jnp.float32)
-            for c in range(0, tokens, chunk):
-                e = jnp.exp2((keep[c : c + chunk, :] - best) * factor)
-                total += jnp.sum(e, axis=0, keepdims=True)
-                accum += jnp.dot(
-                    v_ref[head, :, c : c + chunk], e.astype(jnp.bfloat16), preferred_element_type=jnp.float32
-                )
-            own_ref[slot, head, :, lanes] = (accum / total).astype(jnp.bfloat16)
-            own_log_ref[slot, head, :, lanes] = best * factor + jnp.log2(total)
+    def decode(u):
+        group = u // blocks
+        own = jnp.logical_or(group == 4, group == 7)
+        kind = jnp.where(own, 3, jnp.where(group < 2, 0, jnp.where(group < 4, 1, 2)))
+        head = jnp.where(group < 4, lax.rem(group, 2), jnp.where(own, (group - 4) // 3, group - 5))
+        source = jnp.where(
+            kind == 0, mate, jnp.where(kind == 1, near_over, jnp.where(kind == 2, far_end, me))
+        )
+        return kind, head, lax.rem(u, blocks), source
+
+    chunk = 512
+
+    def score(u, keep_ref, top_ref):
+        _, head, block, source = decode(u)
+        q = asks_ref[source, head, pl.ds(pl.multiple_of(block * BLOCK, BLOCK), BLOCK), :]
+        best = None
+        for c in range(0, tokens, chunk):
+            s = lax.dot_general(
+                k_ref[head, c : c + chunk, :],
+                q,
+                (((1,), (1,)), ((), ())),
+                preferred_element_type=jnp.float32,
+            )
+            keep_ref[c : c + chunk, :] = s
+            top = jnp.max(s, axis=0, keepdims=True)
+            best = top if best is None else jnp.maximum(best, top)
+        top_ref[...] = best
+
+    def weigh(u, keep_ref, top_ref):
+        kind, head, block, _ = decode(u)
+        best = top_ref[...]
+        total = jnp.zeros((1, BLOCK), jnp.float32)
+        accum = jnp.zeros((width, BLOCK), jnp.float32)
+        for c in range(0, tokens, chunk):
+            e = jnp.exp2((keep_ref[c : c + chunk, :] - best) * factor)
+            total += jnp.sum(e, axis=0, keepdims=True)
+            accum += jnp.dot(
+                v_ref[head, :, c : c + chunk], e.astype(jnp.bfloat16), preferred_element_type=jnp.float32
+            )
+        own_ref[kind, head, block] = (accum / total).astype(jnp.bfloat16)
+        own_log_ref[kind, head, block] = best * factor + jnp.log2(total)
 
     def both(src, src_log, dst, dst_log, send, recv, other):
         return (
@@ -521,36 +593,39 @@
             copy(src_log, dst_log, send.at[1], recv.at[1], other),
         )
 
-    def half_copy(j):
+    def half_copy(kind, head, block):
+        at = (kind, head, block)
         return both(
-            own_ref.at[j + 1, 1 - mine],
-            own_log_ref.at[j + 1, 1 - mine],
-            half_ref.at[j],
-            half_log_ref.at[j],
-            half_send.at[j],
-            half_recv.at[j],
+            own_ref.at[at],
+            own_log_ref.at[at],
+            half_ref.at[at],
+            half_log_ref.at[at],
+            half_send.at[at],
+            half_recv.at[at],
             mate,
         )
 
-    def over_copy(j):
+    def over_copy(j, head, block):
+        at = (j, head, block)
         return both(
-            merged_ref.at[j],
-            merged_log_ref.at[j],
-            over_ref.at[mine],
-            over_log_ref.at[mine],
-            over_send.at[j],
-            over_recv.at[mine],
-            near_over if j == 0 else far_end,
-        )
-
-    def mate_copy(head):
+            merged_ref.at[at],
+            merged_log_ref.at[at],
+            over_ref.at[at],
+            over_log_ref.at[at],
+            over_send.at[at],
+            over_recv.at[at],
+            near_over,
+        )
+
+    def last_copy(head, block):
+        at = (head, block)
         return both(
-            own_ref.at[3, head],
-            own_log_ref.at[3, head],
-            mate_ref.at[head],
-            mate_log_ref.at[head],
-            mate_send.at[head],
-            mate_recv.at[head],
+            ready_ref.at[at],
+            ready_log_ref.at[at],
+            last_ref.at[at],
+            last_log_ref.at[at],
+            last_send.at[at],
+            last_recv.at[at],
             mate,
         )
 
@@ -563,101 +638,130 @@
         )
         return mixed, best + jnp.log2(total)
 
-    def merge_half(j):
-        for each in half_copy(j):
+    def merge_half(kind, head, block):
+        for each in half_copy(kind, head, block):
             each.wait_recv()
+        at = (kind - 1, head, block)
         mixed, log = blend(
-            [own_ref[j + 1, mine], half_ref[j]], [own_log_ref[j + 1, mine], half_log_ref[j]]
-        )
-        merged_ref[j] = mixed.astype(jnp.bfloat16)
-        merged_log_ref[j] = log
-        for each in over_copy(j):
+            [own_ref[kind, head, block], half_ref[kind, head, block]],
+            [own_log_ref[kind, head, block], half_log_ref[kind, head, block]],
+        )
+        merged_ref[at] = mixed.astype(jnp.bfloat16)
+        merged_log_ref[at] = log
+        for each in over_copy(*at):
             each.start()
 
-    def serve(u, carry):
-        slot = u // heads
-        second = lax.rem(u, heads)
-        head = jnp.where(second == 0, 1 - mine, mine)
-        source = jnp.where(
-            slot == 0, me, jnp.where(slot == 1, near_over, jnp.where(slot == 2, far_end, mate))
-        )
-
-        @pl.when(
-            jnp.logical_and(
-                jnp.logical_and(second == 0, jnp.logical_not(inside)),
-                jnp.logical_or(slot == 1, slot == 2),
-            )
-        )
+    group_size = heads * blocks
+    lag = 5
+
+    def await_ask(u):
+        kind, head, block, source = decode(u)
+        fresh = jnp.logical_and(block == 0, jnp.logical_or(kind == 1, kind == 2))
+
+        @pl.when(jnp.logical_and(fresh, jnp.logical_not(inside)))
         def _():
-            ask_copy(source, 1 - out_side).wait_recv()
-
-        attend_one(slot, source, head)
-        for j in range(2):
-
-            @pl.when(u == (j + 1) * heads)
+            ask_copy(source, head, 1 - outward).wait_recv()
+
+    def send_on(u):
+        kind, head, block, _ = decode(u)
+
+        @pl.when(jnp.logical_and(kind < 3, jnp.logical_not(inside)))
+        def _():
+            for each in half_copy(kind, head, block):
+                each.start()
+
+        for kind, first in ((1, group_size), (2, group_size + group_size + blocks)):
+            k = u - first - lag
+
+            @pl.when(jnp.logical_and(inside, jnp.logical_and(k >= 0, k < group_size)))
             def _():
-                for each in half_copy(j):
-                    each.start()
-
-            @pl.when(u == (j + 2) * heads)
-            def _():
-                merge_half(j)
-
-        @pl.when(slot == 3)
+                merge_half(kind, k // blocks, lax.rem(k, blocks))
+
+    score(0, even_ref, even_top_ref)
+    units = 4 * group_size
+
+    def serve(i, carry):
+        u = 2 * i
+
+        @pl.when(i == 0)
         def _():
-            for each in mate_copy(head):
-                each.start()
-
+            hand_on(1)
+
+        @pl.when(jnp.logical_and(inside, i == group_size // 2))
+        def _():
+            hand_far(0)
+
+        @pl.when(jnp.logical_and(inside, i == group_size - 1))
+        def _():
+            hand_far(1)
+
+        await_ask(u + 1)
+        score(u + 1, odd_ref, odd_top_ref)
+        weigh(u, even_ref, even_top_ref)
+        send_on(u)
+        ahead = jnp.minimum(u + 2, units - 1)
+        await_ask(ahead)
+        score(ahead, even_ref, even_top_ref)
+        weigh(u + 1, odd_ref, odd_top_ref)
+        send_on(u + 1)
         return carry
 
-    lax.fori_loop(0, 4 * heads, serve, 0)
-
-    for head in range(heads):
-        for each in both(
-            merged_ref.at[0],
-            merged_log_ref.at[0],
-            over_ref.at[head],
-            over_log_ref.at[head],
-            over_send.at[0],
-            over_recv.at[head],
-            near_over,
-        ):
-            each.wait_recv()
-    for head in range(heads):
-        for each in mate_copy(head):
-            each.wait_recv()
-    for head in range(heads):
-        mixed, _ = blend(
-            [own_ref[0, head], over_ref[head], mate_ref[head]],
-            [own_log_ref[0, head], over_log_ref[head], mate_log_ref[head]],
-        )
-        out_ref[head] = mixed.T.astype(out_ref.dtype)
-
-    for side, there in enumerate((has_left, has_right)):
-
-        @pl.when(there)
-        def _():
-            first_copy(side).wait_send()
-            near_copy(side).wait_send()
-
-    for other in range(count):
-
-        @pl.when(far_from(other))
-        def _():
-            far_copy(other).wait_send()
+    lax.fori_loop(0, units // 2, serve, 0)
 
     @pl.when(inside)
     def _():
-        ask_copy(me - 1, 1).wait_send()
-        ask_copy(me + 1, 0).wait_send()
-        ask_copy(far_end, out_side).wait_send()
-
-    for j in range(2):
-        for each in half_copy(j) + over_copy(j):
-            each.wait_send()
+        for k in range(units - (2 * group_size + blocks + lag), group_size):
+            merge_half(2, k // blocks, k % blocks)
+        for head in range(heads):
+            for block in range(blocks):
+                for each in over_copy(1, head, block):
+                    each.wait_recv()
+                mixed, log = blend(
+                    [own_ref[0, head, block], over_ref[1, head, block]],
+                    [own_log_ref[0, head, block], over_log_ref[1, head, block]],
+                )
+                ready_ref[head, block] = mixed.astype(jnp.bfloat16)
+                ready_log_ref[head, block] = log
+                for each in last_copy(head, block):
+                    each.start()
+        for head in range(heads):
+            for block in range(blocks):
+                for each in half_copy(0, head, block) + over_copy(0, head, block):
+                    each.wait_recv()
+                mixed, _ = blend(
+                    [own_ref[3, head, block], half_ref[0, head, block], over_ref[0, head, block]],
+                    [own_log_ref[3, head, block], half_log_ref[0, head, block], over_log_ref[0, head, block]],
+                )
+                out_ref[head, block * BLOCK : (block + 1) * BLOCK, :] = mixed.T.astype(out_ref.dtype)
+        for head in range(heads):
+            ask_copy(me - 1, head, 1).wait_send()
+            ask_copy(me + 1, head, 0).wait_send()
+            ask_copy(far_end, head, outward).wait_send()
+            for block in range(blocks):
+                for each in over_copy(0, head, block) + over_copy(1, head, block) + last_copy(head, block):
+                    each.wait_send()
+
+    @pl.when(jnp.logical_not(inside))
+    def _():
+        for head in range(heads):
+            for block in range(blocks):
+                for each in last_copy(head, block):
+                    each.wait_recv()
+                mixed, _ = blend(
+                    [own_ref[3, head, block], last_ref[head, block]],
+                    [own_log_ref[3, head, block], last_log_ref[head, block]],
+                )
+                out_ref[head, block * BLOCK : (block + 1) * BLOCK, :] = mixed.T.astype(out_ref.dtype)
+        for kind in range(3):
+            for head in range(heads):
+                for block in range(blocks):
+                    for each in half_copy(kind, head, block):
+                        each.wait_send()
+
     for head in range(heads):
-        for each in mate_copy(head):
-            each.wait_send()
+        for_sides(lambda side: ask_copy(me, head, side).wait_send())
+    for_sides(lambda side: near_copy(side).wait_send())
+    for_far(lambda other: far_copy(other).wait_send())
 
 
 def by_tokens(keys, values, queries, positions, count):
@@ -669,24 +773,48 @@
     def tall(matrix):
         return np.concatenate(split_two(matrix), axis=-2)
 
+    def table(places):
+        return tall(np.concatenate(spins(places, width).astype(np.float64), axis=1))
+
     up_high, up_low = split_two(up)
     t_part = near.shape[0]
-    rotated = rotate_rows(queries.astype(jnp.float32), positions.astype(jnp.float32)).astype(
-        jnp.bfloat16
-    )
-    asked = rotated.swapaxes(1, 2)
     tokens = n_dev // 2
-    coarse = spins(np.arange(count * PARTS) * float(t_part), width)
-    fine = spins(np.arange(t_part) * 1.0, width)
-    vmem = pl.BlockSpec(memory_space=pltpu.VMEM)
+    blocks = rows // BLOCK
+    split = 128
+    operands = (
+        table(np.arange(length // split) * float(split)),
+        table(np.arange(split) * 1.0),
+        tall(near),
+        tall(down),
+        np.concatenate([up_high, up_high, up_low], axis=1),
+        tall(local),
+        tall(merge),
+        tall(cross),
+        spins(np.arange(count * PARTS) * float(t_part), width),
+        spins(np.arange(t_part) * 1.0, width),
+    )
+    held = [jax.ShapeDtypeStruct(o.shape[1:] if o.ndim == 3 and o.shape[0] == count else o.shape, o.dtype) for o in operands]
     dma = pltpu.SemaphoreType.DMA
+
+    def parts(*lead):
+        return [
+            pltpu.VMEM(lead + (heads, blocks, width, BLOCK), jnp.bfloat16),
+            pltpu.VMEM(lead + (heads, blocks, 1, BLOCK), jnp.float32),
+        ]
+
     return pl.pallas_call(
         functools.partial(fused_kernel, count, math.log2(math.e) / math.sqrt(width)),
-        in_specs=[vmem] * 8 + [pl.BlockSpec(memory_space=pl.ANY)] + [vmem] * 2,
-        out_specs=vmem,
+        in_specs=[pl.BlockSpec(memory_space=pl.ANY)] * 14,
+        out_specs=pl.BlockSpec(memory_space=pltpu.VMEM),
         out_shape=jax.ShapeDtypeStruct(queries.shape, jnp.bfloat16),
         scratch_shapes=[
-            pltpu.VMEM((2 * cross.shape[1], cross.shape[2]), jnp.bfloat16),
+            pltpu.VMEM(keys.shape, keys.dtype),
+            pltpu.VMEM(values.shape, values.dtype),
+            pltpu.VMEM(queries.shape, queries.dtype),
+            pltpu.VMEM((1, rows), jnp.int32),
+        ]
+        + [pltpu.VMEM(h.shape, h.dtype) for h in held]
+        + [
             pltpu.VMEM((PARTS * ORDER, 2 * columns), jnp.float32),
             pltpu.VMEM((ORDER + FAR, 2 * columns), jnp.float32),
             pltpu.VMEM((cross.shape[2], 2 * columns), jnp.float32),
@@ -694,46 +822,36 @@
             pltpu.VMEM((PARTS * ORDER, 2 * columns), jnp.float32),
             pltpu.VMEM((heads, tokens, width), jnp.bfloat16),
             pltpu.VMEM((heads, width, tokens), jnp.bfloat16),
-            pltpu.VMEM((2, tokens, BLOCK), jnp.float32),
-            pltpu.VMEM((count, heads, width, rows), jnp.bfloat16),
-            pltpu.VMEM((4, heads, width, rows), jnp.bfloat16),
-            pltpu.VMEM((4, heads, 1, rows), jnp.float32),
-            pltpu.VMEM((2, width, rows), jnp.bfloat16),
-            pltpu.VMEM((2, 1, rows), jnp.float32),
-            pltpu.VMEM((2, width, rows), jnp.bfloat16),
-            pltpu.VMEM((2, 1, rows), jnp.float32),
-            pltpu.VMEM((heads, width, rows), jnp.bfloat16),
-            pltpu.VMEM((heads, 1, rows), jnp.float32),
-            pltpu.VMEM((heads, width, rows), jnp.bfloat16),
-            pltpu.VMEM((heads, 1, rows), jnp.float32),
-            dma,
+            pltpu.VMEM((tokens, BLOCK), jnp.float32),
+            pltpu.VMEM((tokens, BLOCK), jnp.float32),
+            pltpu.VMEM((1, BLOCK), jnp.float32),
+            pltpu.VMEM((1, BLOCK), jnp.float32),
+            pltpu.VMEM((count, heads, rows, width), jnp.bfloat16),
+        ]
+        + parts(4)
+        + parts(3)
+        + parts(2)
+        + parts(2)
+        + parts()
+        + parts()
+        + [
+            dma((12,)),
+            dma((PARTS, 2)),
             dma((count,)),
             dma((count,)),
-            dma((count, 2)),
-            dma((count,)),
-            dma((2, 2)),
-            dma((2, 2)),
-            dma((2, 2)),
-            dma((heads, 2)),
-            dma((heads, 2)),
-            dma((heads, 2)),
+            dma((count, heads, 2)),
+            dma((count, heads)),
+            dma((3, heads, blocks, 2)),
+            dma((3, heads, blocks, 2)),
+            dma((2, heads, blocks, 2)),
+            dma((2, heads, blocks, 2)),
+            dma((heads, blocks, 2)),
+            dma((heads, blocks, 2)),
         ],
         compiler_params=pltpu.CompilerParams(
             collective_id=0, has_side_effects=True, vmem_limit_bytes=60 * 1024 * 1024
         ),
-    )(
-        keys,
-        values,
-        asked,
-        tall(near),
-        tall(down),
-        np.concatenate([up_high, up_high, up_low], axis=1),
-        tall(local),
-        tall(merge),
-        tall(cross),
-        coarse,
-        fine,
-    )
+    )(keys, values, queries, positions.reshape(1, rows), *operands)
 
 
 def by_columns(keys, values, queries, positions):
@@ -760,7 +878,7 @@
 
     def on_device(keys, values, queries, positions):
         heads, rows, width = queries.shape
-        if count == 4 and heads == 2 and keys.shape[0] % (PARTS * 512) == 0 and rows % BLOCK == 0:
+        if count == 4 and heads == 2 and keys.shape[0] % (PARTS * 512) == 0 and rows % BLOCK == 0 and width == 128:
             return by_tokens(keys, values, queries, positions, count)
         return by_columns(keys, values, queries, positions)
 

time: 77.2 us -> 60 us (0.78)
  Pallas kernels: 71.7 us -> 56.8 us
  other arithmetic: 2.38 us -> 0 us
    pallas_call x1, Pallas kernels: 71.7 us -> 56.8 us  [by_tokens(): pl.pallas_call(functools.partial(fused_kernel, count, math.log2(math.e) /...]
    reshape x0 -> x1, local copies, waits for them, and re-layouts: none -> 1.27 us  [by_tokens(): positions.reshape(1, rows)]
    unnamed x2 -> x1, local copies, waits for them, and re-layouts: 2.94 us -> 1.77 us
    transpose x1 -> x0, other arithmetic: 0.77 us -> none  [by_tokens(): asked = rotated.swapaxes(1, 2)]
where the time goes in v3:
time: 60 us; the launch traced here: 59.8 us
  Pallas kernels  56.8 us (95%)
  local copies, waits for them, and re-layouts  3.03 us (5%)
    pallas_call x1, Pallas kernels, by_tokens(): pl.pallas_call(functools.partial(fused_kernel, count, math.log2(math.e) /...  56.8 us
    unnamed x1, local copies, waits for them, and re-layouts  1.77 us
    reshape x1, local copies, waits for them, and re-layouts, by_tokens(): positions.reshape(1, rows)  1.27 us

profile of v3, /device:TPU:0, one launch (start us, length us, event | category | flops | bytes accessed | tf_op | source)
XLA Modules:
  0.0 59.8 jit_solution(2828418489830014657)
XLA Ops:
  0.0 1.3 %reshape.3.places_hbm = s32[1,768]{1,0:T(1,128)} reshape(s32[768]{0:T(1024)} %param.17) | data formatting | bytes 6144 | tf_op jit(solution)/shard_map/reshape | solution.py:854
  1.3 56.8 %shard_map.136 = bf16[2,768,128]{2,1,0:T(8,128)(2,1)} custom-call(bf16[4096,256]{1,0:T(8,128)(2,1)} %keys_hbm.1, bf16[4096,256]{1,0:T(8,128)(2,1)} %values_hbm.1, bf16[2,768,128]{2,1,0:T(8,128)(2,1)} %queries_hbm.1, s32[1,768]{1,0:T(1,128)} %reshape.3.places_hbm, bf16[256,256]{1,0:T(8,128)(2,1)} %constant.20.clone.high_hbm, ...), custom_call_target="tpu_custom_call" | custom-call | tf_op jit(solution)/shard_map/pallas_call | solution.py:805
  58.0 1.8 %copy.16 = bf16[2,768,128]{2,1,0:T(8,128)(2,1)} copy(bf16[2,768,128]{2,1,0:T(8,128)(2,1)} %shard_map.136) | data formatting | bytes 786432

commit v4 on v3

--- a/solution.py
+++ b/solution.py
@@ -390,7 +390,7 @@
     split = low_ref.shape[0] // 2
     for i in range(rows // split):
         here = slice(i * split, (i + 1) * split)
-        place = jnp.broadcast_to(places_ref[:, here].astype(jnp.float32), (split, split)).T.astype(jnp.int32)
+        place = jnp.broadcast_to(places_ref[here].astype(jnp.float32)[None], (split, split)).T.astype(jnp.int32)
         spun = []
         for value, table_ref in ((place // split, high_ref), (lax.rem(place, split), low_ref)):
             size = table_ref.shape[0] // 2
@@ -488,36 +488,39 @@
 
     for_sides(lambda side: near_copy(side).start())
     for_far(lambda other: far_copy(other).start())
-    for_sides(lambda side: ask_copy(me, 1, side).start())
+
+    @pl.when(jnp.logical_not(inside))
+    def _():
+        ask_copy(me, 1, 1 - outward).start()
 
     loads[6].wait()
 
     def close(p, carry):
-        start = pl.multiple_of(p * n_part, n_part)
+        start = p * n_part if isinstance(p, int) else pl.multiple_of(p * n_part, n_part)
         for side, (_, x_ref) in enumerate(sides):
             z = jnp.dot(near_ref[...], x_ref[pl.ds(start, n_part), :], preferred_element_type=jnp.float32)
             close_ref[p, :, side * half_columns : (side + 1) * half_columns] = z[:t_part] + z[t_part:]
         return carry
 
-    lax.fori_loop(0, PARTS, close, 0)
+    close(0, 0)
+
+    @pl.when(inside)
+    def _():
+        for side in range(2):
+            ask_copy(me + 2 * side - 1, 0, 1 - side).wait_recv()
+            ask_copy(me + 2 * side - 1, 0, 1 - side).start()
+        ask_copy(me, 1, outward).start()
+
+    lax.fori_loop(1, PARTS, close, 0)
     for each in loads[7:]:
         each.wait()
     field_ref[...] = strict_dot(local_ref[...], parts_ref[...])
 
-    def hand_on(head):
-        for_sides(lambda side: ask_copy(me + 2 * side - 1, head, 1 - side).wait_recv())
-
-        @pl.when(inside)
-        def _():
-            ask_copy(me - 1, head, 1).start()
-            ask_copy(me + 1, head, 0).start()
-
-    def hand_far(head):
-        handed = ask_copy(far_end, head, outward)
+    def hand(source, head, side):
+        handed = ask_copy(source, head, side)
         handed.wait_recv()
         handed.start()
 
-    hand_on(0)
     for_sides(near_wait)
     for_far(far_wait)
     field_ref[...] += strict_dot(cross_ref[...], others_ref[...])
@@ -545,15 +548,36 @@
 
     lax.fori_loop(0, PARTS, finish, 0)
 
+    @pl.when(inside)
+    def _():
+        hand(mate, 1, 1 - outward)
+        ask_copy(me, 1, 1 - outward).start()
+
+    runs = [
+        (0, 0, 0, blocks),
+        (1, 0, 0, blocks),
+        (0, 1, 0, blocks),
+        (3, 0, 0, blocks),
+        (2, 0, 0, blocks),
+        (3, 1, 0, blocks - 1),
+        (2, 1, 0, blocks),
+        (3, 1, blocks - 1, 1),
+        (1, 1, 0, blocks),
+    ]
+    begins = [sum(run[3] for run in runs[:i]) for i in range(len(runs))]
+    units = begins[-1] + blocks
+
     def decode(u):
-        group = u // blocks
-        own = jnp.logical_or(group == 4, group == 7)
-        kind = jnp.where(own, 3, jnp.where(group < 2, 0, jnp.where(group < 4, 1, 2)))
-        head = jnp.where(group < 4, lax.rem(group, 2), jnp.where(own, (group - 4) // 3, group - 5))
+        kind, head, block = runs[0][0], runs[0][1], u
+        for begin, run in zip(begins[1:], runs[1:]):
+            late = u >= begin
+            kind = jnp.where(late, run[0], kind)
+            head = jnp.where(late, run[1], head)
+            block = jnp.where(late, u - begin + run[2], block)
         source = jnp.where(
             kind == 0, mate, jnp.where(kind == 1, near_over, jnp.where(kind == 2, far_end, me))
         )
-        return kind, head, lax.rem(u, blocks), source
+        return kind, head, block, source
 
     chunk = 512
 
@@ -651,16 +675,14 @@
         for each in over_copy(*at):
             each.start()
 
-    group_size = heads * blocks
-    lag = 5
-
     def await_ask(u):
         kind, head, block, source = decode(u)
-        fresh = jnp.logical_and(block == 0, jnp.logical_or(kind == 1, kind == 2))
-
-        @pl.when(jnp.logical_and(fresh, jnp.logical_not(inside)))
+
+        @pl.when(jnp.logical_and(jnp.logical_and(block == 0, kind < 3), jnp.logical_not(inside)))
         def _():
             ask_copy(source, head, 1 - outward).wait_recv()
+
+    lag = 6
 
     def send_on(u):
         kind, head, block, _ = decode(u)
@@ -670,37 +692,34 @@
             for each in half_copy(kind, head, block):
                 each.start()
 
-        for kind, first in ((1, group_size), (2, group_size + group_size + blocks)):
+        for kind, first in ((1, begins[1]), (2, begins[4])):
             k = u - first - lag
 
-            @pl.when(jnp.logical_and(inside, jnp.logical_and(k >= 0, k < group_size)))
+            @pl.when(jnp.logical_and(inside, jnp.logical_and(k >= 0, k < blocks)))
             def _():
-                merge_half(kind, k // blocks, lax.rem(k, blocks))
-
-    score(0, even_ref, even_top_ref)
-    units = 4 * group_size
+                merge_half(kind, 0, k)
+
+    await_ask(jnp.int32(0))
+    score(jnp.int32(0), even_ref, even_top_ref)
 
     def serve(i, carry):
         u = 2 * i
-
-        @pl.when(i == 0)
-        def _():
-            hand_on(1)
-
-        @pl.when(jnp.logical_and(inside, i == group_size // 2))
-        def _():
-            hand_far(0)
-
-        @pl.when(jnp.logical_and(inside, i == group_size - 1))
-        def _():
-            hand_far(1)
+        for at, source, head in ((1, far_end, 0), (4, far_end, 1), (7, near_over, 1)):
+
+            @pl.when(jnp.logical_and(inside, i == at))
+            def _():
+                hand(source, head, outward)
 
         await_ask(u + 1)
         score(u + 1, odd_ref, odd_top_ref)
         weigh(u, even_ref, even_top_ref)
         send_on(u)
         ahead = jnp.minimum(u + 2, units - 1)
-        await_ask(ahead)
+
+        @pl.when(u + 2 < units)
+        def _():
+            await_ask(ahead)
+
         score(ahead, even_ref, even_top_ref)
         weigh(u + 1, odd_ref, odd_top_ref)
         send_on(u + 1)
@@ -708,22 +727,26 @@
 
     lax.fori_loop(0, units // 2, serve, 0)
 
+    def pass_on(head, block):
+        for each in over_copy(1, head, block):
+            each.wait_recv()
+        mixed, log = blend(
+            [own_ref[0, head, block], over_ref[1, head, block]],
+            [own_log_ref[0, head, block], over_log_ref[1, head, block]],
+        )
+        ready_ref[head, block] = mixed.astype(jnp.bfloat16)
+        ready_log_ref[head, block] = log
+        for each in last_copy(head, block):
+            each.start()
+
     @pl.when(inside)
     def _():
-        for k in range(units - (2 * group_size + blocks + lag), group_size):
-            merge_half(2, k // blocks, k % blocks)
-        for head in range(heads):
-            for block in range(blocks):
-                for each in over_copy(1, head, block):
-                    each.wait_recv()
-                mixed, log = blend(
-                    [own_ref[0, head, block], over_ref[1, head, block]],
-                    [own_log_ref[0, head, block], over_log_ref[1, head, block]],
-                )
-                ready_ref[head, block] = mixed.astype(jnp.bfloat16)
-                ready_log_ref[head, block] = log
-                for each in last_copy(head, block):
-                    each.start()
+        for block in range(blocks):
+            merge_half(2, 1, block)
+            pass_on(0, block)
+        for block in range(blocks):
+            pass_on(1, block)
+            merge_half(1, 1, block)
         for head in range(heads):
             for block in range(blocks):
                 for each in half_copy(0, head, block) + over_copy(0, head, block):
@@ -811,7 +834,7 @@
             pltpu.VMEM(keys.shape, keys.dtype),
             pltpu.VMEM(values.shape, values.dtype),
             pltpu.VMEM(queries.shape, queries.dtype),
-            pltpu.VMEM((1, rows), jnp.int32),
+            pltpu.VMEM((rows,), jnp.int32),
         ]
         + [pltpu.VMEM(h.shape, h.dtype) for h in held]
         + [
@@ -851,7 +874,7 @@
         compiler_params=pltpu.CompilerParams(
             collective_id=0, has_side_effects=True, vmem_limit_bytes=60 * 1024 * 1024
         ),
-    )(keys, values, queries, positions.reshape(1, rows), *operands)
+    )(keys, values, queries, positions, *operands)
 
 
 def by_columns(keys, values, queries, positions):

time: 60 us -> 55.4 us (0.923)
  Pallas kernels: 56.8 us -> 53.5 us
  local copies, waits for them, and re-layouts: 3.03 us -> 1.77 us
    pallas_call x1, Pallas kernels: 56.8 us -> 53.5 us  [by_tokens(): pl.pallas_call(functools.partial(fused_kernel, count, math.log2(math.e) /...]
    reshape x1 -> x0, local copies, waits for them, and re-layouts: 1.27 us -> none  [by_tokens(): positions.reshape(1, rows)]
where the time goes in v4:
time: 55.4 us; the launch traced here: 55.2 us
  Pallas kernels  53.5 us (97%)
  local copies, waits for them, and re-layouts  1.77 us (3%)
    pallas_call x1, Pallas kernels, by_tokens(): pl.pallas_call(functools.partial(fused_kernel, count, math.log2(math.e) /...  53.5 us
    unnamed x1, local copies, waits for them, and re-layouts  1.77 us

profile of v4, /device:TPU:0, one launch (start us, length us, event | category | flops | bytes accessed | tf_op | source)
XLA Modules:
  0.0 55.2 jit_solution(10348344201706286834)
XLA Ops:
  0.0 53.5 %shard_map.136 = bf16[2,768,128]{2,1,0:T(8,128)(2,1)} custom-call(bf16[4096,256]{1,0:T(8,128)(2,1)} %keys_hbm.1, bf16[4096,256]{1,0:T(8,128)(2,1)} %values_hbm.1, bf16[2,768,128]{2,1,0:T(8,128)(2,1)} %queries_hbm.1, s32[768]{0:T(1024)} %places_hbm.1, bf16[256,256]{1,0:T(8,128)(2,1)} %constant.20.clone.high_hbm, bf16[256,256]{1,0:T(8,128)(2,1)} %constant.21.clone.low_hbm, ...), custom_call_target="tpu_custom_call" | custom-call | tf_op jit(solution)/shard_map/pallas_call | solution.py:828
  53.5 1.8 %copy.16 = bf16[2,768,128]{2,1,0:T(8,128)(2,1)} copy(bf16[2,768,128]{2,1,0:T(8,128)(2,1)} %shard_map.136) | data formatting | bytes 786432

commit v5 on v4

--- a/solution.py
+++ b/solution.py
@@ -12,6 +12,7 @@
 OUTER = 128
 PARTS = 4
 ORDER = 64
+EDGE = 32
 FAR = 16
 BLOCK = 256
 MESH = pl.DeviceIdType.MESH
@@ -178,15 +179,20 @@
     )(swap.reshape(1), queries, keys, values, *state)
 
 
-def nodes(count, order, pad):
-    half = np.log((count - 1 + pad) / pad)
-    e = np.exp(half * np.cos(np.pi * (2 * np.arange(order) + 1) / (2 * order)))
-    return ((count - 1 + pad) * e - pad) / (1 + e)
-
-
-def cardinals(places, count, order, pad):
-    half = np.log((count - 1 + pad) / pad)
-    at = np.arccos(np.clip(np.log((places + pad) / (count - 1 + pad - places)) / half, -1.0, 1.0))
+def bounds(count, left, right):
+    return np.log(left / (count - 1 + right)), np.log((count - 1 + left) / right)
+
+
+def nodes(count, order, left, right):
+    low, top = bounds(count, left, right)
+    e = np.exp((top - low) / 2 * np.cos(np.pi * (2 * np.arange(order) + 1) / (2 * order)) + (top + low) / 2)
+    return ((count - 1 + right) * e - left) / (1 + e)
+
+
+def cardinals(places, count, order, left, right):
+    low, top = bounds(count, left, right)
+    at = (2 * np.log((places + left) / (count - 1 + right - places)) - top - low) / (top - low)
+    at = np.arccos(np.clip(at, -1.0, 1.0))
     own = np.pi * (2 * np.arange(order) + 1) / (2 * order)
     total = np.zeros((places.size, order))
     for k in range(order):
@@ -209,35 +215,40 @@
     sign_n = np.array([1.0, -1.0, -1.0, 1.0])[n % 4]
     sign_t = np.where(t % 2 == 0, 1.0, -1.0)
     near = sign_t[:, None] * sign_n * scale * cot(4 * t[:, None] - 2 * n + 1.0)
-    down = cardinals(n, n_part, order, 1.5).T * sign_n
-    up = sign_t[:, None] * cardinals(t, t_part, order, 0.75)
+    down = cardinals(n, n_part, order, 1.5, 1.5).T * sign_n
+    up = sign_t[:, None] * cardinals(t, t_part, order, 0.75, 0.75)
     part = np.arange(parts)[:, None]
-    source = (part * n_part + nodes(n_part, order, 1.5)).reshape(-1)
-    target = (part * t_part + nodes(t_part, order, 0.75)).reshape(-1)
-    bend = np.pi * (2 * np.arange(FAR) + 1) / (2 * FAR)
-    spot = np.arccos(np.clip(2.0 * source / (n_dev - 1) - 1.0, -1.0, 1.0))
-    plain = sum(
-        (1.0 if k == 0 else 2.0) / FAR * np.cos(k * bend)[:, None] * np.cos(k * spot)[None, :]
-        for k in range(FAR)
-    )
-    merge = np.concatenate([cardinals(source, n_dev, order, 1.5).T, plain])
+    source = (part * n_part + nodes(n_part, order, 1.5, 1.5)).reshape(-1)
+    target = (part * t_part + nodes(t_part, order, 0.75, 0.75)).reshape(-1)
     own = np.arange(parts * order) // order
     same = own[:, None] == own[None, :]
     local = np.where(same, 0.0, scale * cot(np.where(same, 1.0, 4 * target[:, None] - 2 * source + 1)))
-    whole = nodes(n_dev, order, 1.5)
-    sparse = (np.cos(bend) + 1.0) * (n_dev - 1) / 2
-    cross = np.zeros((devices, parts * order, 3 * order + devices * FAR))
+    last = n_dev - 1
+    wide = float(n_dev)
+    merge = np.concatenate(
+        [
+            cardinals(source, n_dev, EDGE, 1.5, wide).T,
+            cardinals(last - source, n_dev, EDGE, 1.5, wide).T,
+            cardinals(source, n_dev, FAR, 2 * wide, 2 * wide).T,
+        ]
+    )
+    to_left = nodes(n_dev, EDGE, 1.5, wide)
+    sparse = nodes(n_dev, FAR, 2 * wide, 2 * wide)
+    size = 3 * EDGE + devices * FAR
+    cross = np.zeros((devices, parts * order, size + -size % 128))
     for r in range(devices):
         a = 4 * (target + r * t_dev)[:, None]
         for s in range(devices):
-            b = 2 * ((sparse if abs(r - s) > 1 else whole) + s * n_dev)
+            if abs(r - s) > 1:
+                spots, start = sparse, 3 * EDGE + s * FAR
+            elif s < r or (s == r and 2 * r >= devices):
+                spots, start = last - to_left, EDGE * (r - s)
+            else:
+                spots, start = to_left, 2 * EDGE * (s - r)
+            b = 2 * (spots + s * n_dev)
             block = scale * cot(a + b + 3)
             if r != s:
                 block = block + scale * cot(a - b + 1)
-            if abs(r - s) > 1:
-                start = 3 * order + s * FAR
-            else:
-                start = {0: 0, 1: order, -1: 2 * order}[r - s]
             cross[r, :, start : start + block.shape[1]] = block
     return near, down, up, local, merge, cross
 
@@ -309,6 +320,8 @@
     last_log_ref,
     load_sem,
     token_sem,
+    behind_sem,
+    end_sem,
     field_send,
     field_recv,
     ask_send,
@@ -346,12 +359,19 @@
             device_id_type=MESH,
         )
 
+    def for_sides(action):
+        for side, there in enumerate((has_left, has_right)):
+
+            @pl.when(there)
+            def _():
+                action(side)
+
+    def greet(sem, other):
+        pl.semaphore_signal(sem, inc=1, device_id={"ctx": other}, device_id_type=MESH)
+
     others_ref[...] = jnp.zeros_like(others_ref)
     barrier = pltpu.get_barrier_semaphore()
-    for step in range(1, count):
-        pl.semaphore_signal(
-            barrier, inc=1, device_id={"ctx": lax.rem(me + step, count)}, device_id_type=MESH
-        )
+    for_sides(lambda side: greet(barrier, me + 2 * side - 1))
     pairs = (
         (places_hbm, places_ref),
         (queries_hbm, queries_ref),
@@ -407,24 +427,25 @@
             x = queries_ref[head, here, :].astype(jnp.float32)
             asks_ref[me, head, here, :] = (x * cosine + pltpu.roll(x, width // 2, 1) * sine).astype(jnp.bfloat16)
 
-    def ask_copy(source, head, side):
+    def ask_copy(source, head, block, side):
+        here = pl.ds(block * BLOCK if isinstance(block, int) else pl.multiple_of(block * BLOCK, BLOCK), BLOCK)
         return copy(
-            asks_ref.at[source, head],
-            asks_ref.at[source, head],
-            ask_send.at[source, head, side],
-            ask_recv.at[source, head],
+            asks_ref.at[source, head, here],
+            asks_ref.at[source, head, here],
+            ask_send.at[source, head, block, side],
+            ask_recv.at[source, head, block],
             me + 2 * side - 1,
         )
 
-    def for_sides(action):
-        for side, there in enumerate((has_left, has_right)):
-
-            @pl.when(there)
-            def _():
-                action(side)
-
-    pl.semaphore_wait(barrier, count - 1)
-    for_sides(lambda side: ask_copy(me, 0, side).start())
+    pl.semaphore_wait(barrier, jnp.where(inside, 2, 1))
+    for block in range(blocks):
+        for_sides(lambda side: ask_copy(me, 0, block, side).start())
+    for_sides(lambda side: greet(behind_sem.at[1 - side], me + 2 * side - 1))
+    for_sides(lambda side: pl.semaphore_wait(behind_sem.at[side], 1))
+
+    @pl.when(inside)
+    def _():
+        greet(end_sem, mate)
 
     for each in loads[4:6]:
         each.wait()
@@ -438,14 +459,13 @@
                 p * order : (p + 1) * order, side * half_columns : (side + 1) * half_columns
             ] = z[:order] + z[order:]
     whole_ref[...] = strict_dot(merge_ref[...], parts_ref[...])
-    others_ref[:order] = whole_ref[:order]
+    others_ref[:EDGE] = whole_ref[pl.ds(pl.multiple_of(jnp.where(lower, 0, EDGE), EDGE), EDGE), :]
 
     def near_copy(side):
-        start = order * (2 - side)
         other = me + 2 * side - 1
         return copy(
-            whole_ref.at[pl.ds(0, order)],
-            others_ref.at[pl.ds(start, order)],
+            whole_ref.at[pl.ds(side * EDGE, EDGE)],
+            others_ref.at[pl.ds(EDGE * (2 - side), EDGE)],
             field_send.at[other],
             field_recv.at[me],
             other,
@@ -453,8 +473,8 @@
 
     def far_copy(other):
         return copy(
-            whole_ref.at[pl.ds(order, FAR)],
-            others_ref.at[pl.ds(pl.multiple_of(3 * order + me * FAR, FAR), FAR)],
+            whole_ref.at[pl.ds(2 * EDGE, FAR)],
+            others_ref.at[pl.ds(pl.multiple_of(3 * EDGE + me * FAR, FAR), FAR)],
             field_send.at[other],
             field_recv.at[me],
             other,
@@ -463,8 +483,8 @@
     def near_wait(side):
         source = me + 2 * side - 1
         copy(
-            whole_ref.at[pl.ds(0, order)],
-            others_ref.at[pl.ds(order * (1 + side), order)],
+            whole_ref.at[pl.ds(0, EDGE)],
+            others_ref.at[pl.ds(EDGE * (1 + side), EDGE)],
             field_send.at[source],
             field_recv.at[source],
             source,
@@ -472,8 +492,8 @@
 
     def far_wait(source):
         copy(
-            whole_ref.at[pl.ds(order, FAR)],
-            others_ref.at[pl.ds(3 * order + source * FAR, FAR)],
+            whole_ref.at[pl.ds(2 * EDGE, FAR)],
+            others_ref.at[pl.ds(3 * EDGE + source * FAR, FAR)],
             field_send.at[source],
             field_recv.at[source],
             source,
@@ -487,11 +507,17 @@
                 action(other)
 
     for_sides(lambda side: near_copy(side).start())
-    for_far(lambda other: far_copy(other).start())
 
     @pl.when(jnp.logical_not(inside))
     def _():
-        ask_copy(me, 1, 1 - outward).start()
+        pl.semaphore_wait(end_sem, 1)
+
+    for_far(lambda other: far_copy(other).start())
+
+    @pl.when(jnp.logical_not(inside))
+    def _():
+        for block in range(blocks):
+            ask_copy(me, 1, block, 1 - outward).start()
 
     loads[6].wait()
 
@@ -506,10 +532,13 @@
 
     @pl.when(inside)
     def _():
-        for side in range(2):
-            ask_copy(me + 2 * side - 1, 0, 1 - side).wait_recv()
-            ask_copy(me + 2 * side - 1, 0, 1 - side).start()
-        ask_copy(me, 1, outward).start()
+        for block in range(blocks):
+            for side in range(2):
+                handed = ask_copy(me + 2 * side - 1, 0, block, 1 - side)
+                handed.wait_recv()
+                handed.start()
+        for block in range(blocks):
+            ask_copy(me, 1, block, outward).start()
 
     lax.fori_loop(1, PARTS, close, 0)
     for each in loads[7:]:
@@ -517,9 +546,10 @@
     field_ref[...] = strict_dot(local_ref[...], parts_ref[...])
 
     def hand(source, head, side):
-        handed = ask_copy(source, head, side)
-        handed.wait_recv()
-        handed.start()
+        for block in range(blocks):
+            handed = ask_copy(source, head, block, side)
+            handed.wait_recv()
+            handed.start()
 
     for_sides(near_wait)
     for_far(far_wait)
@@ -551,7 +581,8 @@
     @pl.when(inside)
     def _():
         hand(mate, 1, 1 - outward)
-        ask_copy(me, 1, 1 - outward).start()
+        for block in range(blocks):
+            ask_copy(me, 1, block, 1 - outward).start()
 
     runs = [
         (0, 0, 0, blocks),
@@ -678,9 +709,9 @@
     def await_ask(u):
         kind, head, block, source = decode(u)
 
-        @pl.when(jnp.logical_and(jnp.logical_and(block == 0, kind < 3), jnp.logical_not(inside)))
+        @pl.when(jnp.logical_and(kind < 3, jnp.logical_not(inside)))
         def _():
-            ask_copy(source, head, 1 - outward).wait_recv()
+            ask_copy(source, head, block, 1 - outward).wait_recv()
 
     lag = 6
 
@@ -726,6 +757,15 @@
         return carry
 
     lax.fori_loop(0, units // 2, serve, 0)
+
+    def settle(head, block):
+        for each in half_copy(0, head, block) + over_copy(0, head, block):
+            each.wait_recv()
+        mixed, _ = blend(
+            [own_ref[3, head, block], half_ref[0, head, block], over_ref[0, head, block]],
+            [own_log_ref[3, head, block], half_log_ref[0, head, block], over_log_ref[0, head, block]],
+        )
+        out_ref[head, block * BLOCK : (block + 1) * BLOCK, :] = mixed.T.astype(out_ref.dtype)
 
     def pass_on(head, block):
         for each in over_copy(1, head, block):
@@ -745,22 +785,17 @@
             merge_half(2, 1, block)
             pass_on(0, block)
         for block in range(blocks):
+            settle(0, block)
+        for block in range(blocks):
             pass_on(1, block)
             merge_half(1, 1, block)
+        for block in range(blocks):
+            settle(1, block)
         for head in range(heads):
             for block in range(blocks):
-                for each in half_copy(0, head, block) + over_copy(0, head, block):
-                    each.wait_recv()
-                mixed, _ = blend(
-                    [own_ref[3, head, block], half_ref[0, head, block], over_ref[0, head, block]],
-                    [own_log_ref[3, head, block], half_log_ref[0, head, block], over_log_ref[0, head, block]],
-                )
-                out_ref[head, block * BLOCK : (block + 1) * BLOCK, :] = mixed.T.astype(out_ref.dtype)
-        for head in range(heads):
-            ask_copy(me - 1, head, 1).wait_send()
-            ask_copy(me + 1, head, 0).wait_send()
-            ask_copy(far_end, head, outward).wait_send()
-            for block in range(blocks):
+                ask_copy(me - 1, head, block, 1).wait_send()
+                ask_copy(me + 1, head, block, 0).wait_send()
+                ask_copy(far_end, head, block, outward).wait_send()
                 for each in over_copy(0, head, block) + over_copy(1, head, block) + last_copy(head, block):
                     each.wait_send()
 
@@ -782,7 +817,8 @@
                         each.wait_send()
 
     for head in range(heads):
-        for_sides(lambda side: ask_copy(me, head, side).wait_send())
+        for block in range(blocks):
+            for_sides(lambda side: ask_copy(me, head, block, side).wait_send())
     for_sides(lambda side: near_copy(side).wait_send())
     for_far(lambda other: far_copy(other).wait_send())
 
@@ -839,7 +875,7 @@
         + [pltpu.VMEM(h.shape, h.dtype) for h in held]
         + [
             pltpu.VMEM((PARTS * ORDER, 2 * columns), jnp.float32),
-            pltpu.VMEM((ORDER + FAR, 2 * columns), jnp.float32),
+            pltpu.VMEM((2 * EDGE + FAR, 2 * columns), jnp.float32),
             pltpu.VMEM((cross.shape[2], 2 * columns), jnp.float32),
             pltpu.VMEM((PARTS, t_part, 2 * columns), jnp.float32),
             pltpu.VMEM((PARTS * ORDER, 2 * columns), jnp.float32),
@@ -860,10 +896,12 @@
         + [
             dma((12,)),
             dma((PARTS, 2)),
+            pltpu.SemaphoreType.REGULAR((2,)),
+            pltpu.SemaphoreType.REGULAR,
             dma((count,)),
             dma((count,)),
-            dma((count, heads, 2)),
-            dma((count, heads)),
+            dma((count, heads, blocks, 2)),
+            dma((count, heads, blocks)),
             dma((3, heads, blocks, 2)),
             dma((3, heads, blocks, 2)),
             dma((2, heads, blocks, 2)),

time: 55.4 us -> 54.6 us (0.986)
  Pallas kernels: 53.5 us -> 52.7 us
    pallas_call x1, Pallas kernels: 53.5 us -> 52.7 us  [by_tokens(): pl.pallas_call(functools.partial(fused_kernel, count, math.log2(math.e) /...]
where the time goes in v5:
time: 54.6 us; the launch traced here: 54.5 us
  Pallas kernels  52.7 us (97%)
  local copies, waits for them, and re-layouts  1.77 us (3%)
    pallas_call x1, Pallas kernels, by_tokens(): pl.pallas_call(functools.partial(fused_kernel, count, math.log2(math.e) /...  52.7 us
    unnamed x1, local copies, waits for them, and re-layouts  1.77 us

profile of v5, /device:TPU:0, one launch (start us, length us, event | category | flops | bytes accessed | tf_op | source)
XLA Modules:
  0.0 54.5 jit_solution(7968696189703307076)
XLA Ops:
  0.0 52.7 %shard_map.136 = bf16[2,768,128]{2,1,0:T(8,128)(2,1)} custom-call(bf16[4096,256]{1,0:T(8,128)(2,1)} %keys_hbm.1, bf16[4096,256]{1,0:T(8,128)(2,1)} %values_hbm.1, bf16[2,768,128]{2,1,0:T(8,128)(2,1)} %queries_hbm.1, s32[768]{0:T(1024)} %places_hbm.1, bf16[256,256]{1,0:T(8,128)(2,1)} %constant.20.clone.high_hbm, bf16[256,256]{1,0:T(8,128)(2,1)} %constant.21.clone.low_hbm, ...), custom_call_target="tpu_custom_call" | custom-call | tf_op jit(solution)/shard_map/pallas_call | solution.py:864
  52.7 1.8 %copy.16 = bf16[2,768,128]{2,1,0:T(8,128)(2,1)} copy(bf16[2,768,128]{2,1,0:T(8,128)(2,1)} %shard_map.136) | data formatting | bytes 786432

commit v6 on v5

--- a/solution.py
+++ b/solution.py
@@ -537,8 +537,6 @@
                 handed = ask_copy(me + 2 * side - 1, 0, block, 1 - side)
                 handed.wait_recv()
                 handed.start()
-        for block in range(blocks):
-            ask_copy(me, 1, block, outward).start()
 
     lax.fori_loop(1, PARTS, close, 0)
     for each in loads[7:]:
@@ -581,19 +579,20 @@
     @pl.when(inside)
     def _():
         hand(mate, 1, 1 - outward)
+        ask_copy(me, 1, 0, outward).start()
         for block in range(blocks):
             ask_copy(me, 1, block, 1 - outward).start()
 
     runs = [
         (0, 0, 0, blocks),
         (1, 0, 0, blocks),
-        (0, 1, 0, blocks),
         (3, 0, 0, blocks),
         (2, 0, 0, blocks),
         (3, 1, 0, blocks - 1),
         (2, 1, 0, blocks),
         (3, 1, blocks - 1, 1),
         (1, 1, 0, blocks),
+        (0, 1, 0, blocks),
     ]
     begins = [sum(run[3] for run in runs[:i]) for i in range(len(runs))]
     units = begins[-1] + blocks
@@ -713,7 +712,7 @@
         def _():
             ask_copy(source, head, block, 1 - outward).wait_recv()
 
-    lag = 6
+    merges = ((1, 0, begins[1] + 6), (2, 0, begins[3] + 8), (2, 1, begins[5] + 8))
 
     def send_on(u):
         kind, head, block, _ = decode(u)
@@ -723,23 +722,26 @@
             for each in half_copy(kind, head, block):
                 each.start()
 
-        for kind, first in ((1, begins[1]), (2, begins[4])):
-            k = u - first - lag
+        for kind, head, first in merges:
+            k = u - first
 
             @pl.when(jnp.logical_and(inside, jnp.logical_and(k >= 0, k < blocks)))
             def _():
-                merge_half(kind, 0, k)
+                merge_half(kind, head, k)
 
     await_ask(jnp.int32(0))
     score(jnp.int32(0), even_ref, even_top_ref)
 
     def serve(i, carry):
         u = 2 * i
-        for at, source, head in ((1, far_end, 0), (4, far_end, 1), (7, near_over, 1)):
+        for at, source, head in ((1, far_end, 0), (3, far_end, 1), (6, near_over, 1)):
 
             @pl.when(jnp.logical_and(inside, i == at))
             def _():
                 hand(source, head, outward)
+                if source is near_over:
+                    for block in range(1, blocks):
+                        ask_copy(me, 1, block, outward).start()
 
         await_ask(u + 1)
         score(u + 1, odd_ref, odd_top_ref)
@@ -781,8 +783,9 @@
 
     @pl.when(inside)
     def _():
+        for block in range(units - merges[2][2], blocks):
+            merge_half(2, 1, block)
         for block in range(blocks):
-            merge_half(2, 1, block)
             pass_on(0, block)
         for block in range(blocks):
             settle(0, block)

time: 54.6 us -> 52.5 us (0.962)
  Pallas kernels: 52.7 us -> 50.6 us
    pallas_call x1, Pallas kernels: 52.7 us -> 50.6 us  [by_tokens(): pl.pallas_call(functools.partial(fused_kernel, count, math.log2(math.e) /...]
where the time goes in v6:
time: 52.5 us; the launch traced here: 52.3 us
  Pallas kernels  50.6 us (96%)
  local copies, waits for them, and re-layouts  1.77 us (3%)
    pallas_call x1, Pallas kernels, by_tokens(): pl.pallas_call(functools.partial(fused_kernel, count, math.log2(math.e) /...  50.6 us
    unnamed x1, local copies, waits for them, and re-layouts  1.77 us

profile of v6, /device:TPU:0, one launch (start us, length us, event | category | flops | bytes accessed | tf_op | source)
XLA Modules:
  0.0 52.3 jit_solution(6544498492552531313)
XLA Ops:
  0.0 50.6 %shard_map.136 = bf16[2,768,128]{2,1,0:T(8,128)(2,1)} custom-call(bf16[4096,256]{1,0:T(8,128)(2,1)} %keys_hbm.1, bf16[4096,256]{1,0:T(8,128)(2,1)} %values_hbm.1, bf16[2,768,128]{2,1,0:T(8,128)(2,1)} %queries_hbm.1, s32[768]{0:T(1024)} %places_hbm.1, bf16[256,256]{1,0:T(8,128)(2,1)} %constant.20.clone.high_hbm, bf16[256,256]{1,0:T(8,128)(2,1)} %constant.21.clone.low_hbm, ...), custom_call_target="tpu_custom_call" | custom-call | tf_op jit(solution)/shard_map/pallas_call | solution.py:867
  50.6 1.8 %copy.16 = bf16[2,768,128]{2,1,0:T(8,128)(2,1)} copy(bf16[2,768,128]{2,1,0:T(8,128)(2,1)} %shard_map.136) | data formatting | bytes 786432

commit v7 on v5

--- a/solution.py
+++ b/solution.py
@@ -499,6 +499,11 @@
             source,
         ).wait_recv()
 
+    def hand(source, head, block, side):
+        handed = ask_copy(source, head, block, side)
+        handed.wait_recv()
+        handed.start()
+
     def for_far(action):
         for other in range(count):
 
@@ -534,22 +539,19 @@
     def _():
         for block in range(blocks):
             for side in range(2):
-                handed = ask_copy(me + 2 * side - 1, 0, block, 1 - side)
-                handed.wait_recv()
-                handed.start()
-        for block in range(blocks):
-            ask_copy(me, 1, block, outward).start()
+                hand(me + 2 * side - 1, 0, block, 1 - side)
+        ask_copy(me, 1, 0, outward).start()
 
     lax.fori_loop(1, PARTS, close, 0)
+
+    @pl.when(inside)
+    def _():
+        hand(mate, 1, 0, 1 - outward)
+        ask_copy(me, 1, 1, outward).start()
+
     for each in loads[7:]:
         each.wait()
     field_ref[...] = strict_dot(local_ref[...], parts_ref[...])
-
-    def hand(source, head, side):
-        for block in range(blocks):
-            handed = ask_copy(source, head, block, side)
-            handed.wait_recv()
-            handed.start()
 
     for_sides(near_wait)
     for_far(far_wait)
@@ -580,20 +582,22 @@
 
     @pl.when(inside)
     def _():
-        hand(mate, 1, 1 - outward)
+        for block in range(1, blocks):
+            hand(mate, 1, block, 1 - outward)
         for block in range(blocks):
             ask_copy(me, 1, block, 1 - outward).start()
 
     runs = [
         (0, 0, 0, blocks),
         (1, 0, 0, blocks),
-        (0, 1, 0, blocks),
-        (3, 0, 0, blocks),
         (2, 0, 0, blocks),
-        (3, 1, 0, blocks - 1),
+        (0, 1, 0, blocks - 1),
         (2, 1, 0, blocks),
-        (3, 1, blocks - 1, 1),
+        (3, 0, 0, blocks - 1),
         (1, 1, 0, blocks),
+        (0, 1, blocks - 1, 1),
+        (3, 0, blocks - 1, 1),
+        (3, 1, 0, blocks),
     ]
     begins = [sum(run[3] for run in runs[:i]) for i in range(len(runs))]
     units = begins[-1] + blocks
@@ -706,58 +710,6 @@
         for each in over_copy(*at):
             each.start()
 
-    def await_ask(u):
-        kind, head, block, source = decode(u)
-
-        @pl.when(jnp.logical_and(kind < 3, jnp.logical_not(inside)))
-        def _():
-            ask_copy(source, head, block, 1 - outward).wait_recv()
-
-    lag = 6
-
-    def send_on(u):
-        kind, head, block, _ = decode(u)
-
-        @pl.when(jnp.logical_and(kind < 3, jnp.logical_not(inside)))
-        def _():
-            for each in half_copy(kind, head, block):
-                each.start()
-
-        for kind, first in ((1, begins[1]), (2, begins[4])):
-            k = u - first - lag
-
-            @pl.when(jnp.logical_and(inside, jnp.logical_and(k >= 0, k < blocks)))
-            def _():
-                merge_half(kind, 0, k)
-
-    await_ask(jnp.int32(0))
-    score(jnp.int32(0), even_ref, even_top_ref)
-
-    def serve(i, carry):
-        u = 2 * i
-        for at, source, head in ((1, far_end, 0), (4, far_end, 1), (7, near_over, 1)):
-
-            @pl.when(jnp.logical_and(inside, i == at))
-            def _():
-                hand(source, head, outward)
-
-        await_ask(u + 1)
-        score(u + 1, odd_ref, odd_top_ref)
-        weigh(u, even_ref, even_top_ref)
-        send_on(u)
-        ahead = jnp.minimum(u + 2, units - 1)
-
-        @pl.when(u + 2 < units)
-        def _():
-            await_ask(ahead)
-
-        score(ahead, even_ref, even_top_ref)
-        weigh(u + 1, odd_ref, odd_top_ref)
-        send_on(u + 1)
-        return carry
-
-    lax.fori_loop(0, units // 2, serve, 0)
-
     def settle(head, block):
         for each in half_copy(0, head, block) + over_copy(0, head, block):
             each.wait_recv()
@@ -779,28 +731,103 @@
         for each in last_copy(head, block):
             each.start()
 
+    def await_ask(u):
+        kind, head, block, source = decode(u)
+
+        @pl.when(jnp.logical_and(kind < 3, jnp.logical_not(inside)))
+        def _():
+            ask_copy(source, head, block, 1 - outward).wait_recv()
+
+    merges = ((1, 0, begins[1] + 7), (2, 0, begins[2] + 8), (2, 1, begins[4] + 8))
+    passes = begins[2] + 12
+
+    def send_on(u):
+        kind, head, block, _ = decode(u)
+
+        @pl.when(jnp.logical_and(kind < 3, jnp.logical_not(inside)))
+        def _():
+            for each in half_copy(kind, head, block):
+                each.start()
+
+        for kind, head, first in merges:
+            k = u - first
+
+            @pl.when(jnp.logical_and(inside, jnp.logical_and(k >= 0, k < blocks)))
+            def _():
+                merge_half(kind, head, k)
+
+        k = u - passes
+
+        @pl.when(jnp.logical_and(inside, jnp.logical_and(k >= 0, k < blocks)))
+        def _():
+            pass_on(0, k)
+
+    await_ask(jnp.int32(0))
+    score(jnp.int32(0), even_ref, even_top_ref)
+
+    def serve(i, carry):
+        u = 2 * i
+        for at, source, head in ((0, far_end, 0), (3, far_end, 1), (5, near_over, 1)):
+
+            @pl.when(jnp.logical_and(inside, i == at))
+            def _():
+                for block in range(blocks):
+                    hand(source, head, block, outward)
+                if source is near_over:
+                    for block in range(2, blocks):
+                        ask_copy(me, 1, block, outward).start()
+
+        await_ask(u + 1)
+        score(u + 1, odd_ref, odd_top_ref)
+        weigh(u, even_ref, even_top_ref)
+        send_on(u)
+        ahead = jnp.minimum(u + 2, units - 1)
+
+        @pl.when(u + 2 < units)
+        def _():
+            await_ask(ahead)
+
+        score(ahead, even_ref, even_top_ref)
+        weigh(u + 1, odd_ref, odd_top_ref)
+        send_on(u + 1)
+        return carry
+
+    lax.fori_loop(0, units // 2, serve, 0)
+
     @pl.when(inside)
     def _():
         for block in range(blocks):
-            merge_half(2, 1, block)
-            pass_on(0, block)
-        for block in range(blocks):
-            settle(0, block)
-        for block in range(blocks):
             pass_on(1, block)
             merge_half(1, 1, block)
-        for block in range(blocks):
-            settle(1, block)
         for head in range(heads):
             for block in range(blocks):
                 ask_copy(me - 1, head, block, 1).wait_send()
                 ask_copy(me + 1, head, block, 0).wait_send()
                 ask_copy(far_end, head, block, outward).wait_send()
+
+    for head in range(heads):
+        for block in range(blocks):
+            for_sides(lambda side: ask_copy(me, head, block, side).wait_send())
+    for_sides(lambda side: near_copy(side).wait_send())
+    for_far(lambda other: far_copy(other).wait_send())
+
+    @pl.when(inside)
+    def _():
+        for head in range(heads):
+            for block in range(blocks):
+                settle(head, block)
+        for head in range(heads):
+            for block in range(blocks):
                 for each in over_copy(0, head, block) + over_copy(1, head, block) + last_copy(head, block):
                     each.wait_send()
 
     @pl.when(jnp.logical_not(inside))
     def _():
+        for kind in range(3):
+            for head in range(heads):
+                for block in range(blocks):
+                    for each in half_copy(kind, head, block):
+                        each.wait_send()
         for head in range(heads):
             for block in range(blocks):
                 for each in last_copy(head, block):
@@ -810,17 +837,10 @@
                     [own_log_ref[3, head, block], last_log_ref[head, block]],
                 )
                 out_ref[head, block * BLOCK : (block + 1) * BLOCK, :] = mixed.T.astype(out_ref.dtype)
-        for kind in range(3):
-            for head in range(heads):
-                for block in range(blocks):
-                    for each in half_copy(kind, head, block):
-                        each.wait_send()
-
-    for head in range(heads):
-        for block in range(blocks):
-            for_sides(lambda side: ask_copy(me, head, block, side).wait_send())
-    for_sides(lambda side: near_copy(side).wait_send())
-    for_far(lambda other: far_copy(other).wait_send())
+
+
+def hand_out(source_ref, out_ref):
+    out_ref[...] = source_ref[...]
 
 
 def by_tokens(keys, values, queries, positions, count):
@@ -861,7 +881,7 @@
             pltpu.VMEM(lead + (heads, blocks, 1, BLOCK), jnp.float32),
         ]
 
-    return pl.pallas_call(
+    settled = pl.pallas_call(
         functools.partial(fused_kernel, count, math.log2(math.e) / math.sqrt(width)),
         in_specs=[pl.BlockSpec(memory_space=pl.ANY)] * 14,
         out_specs=pl.BlockSpec(memory_space=pltpu.VMEM),
@@ -913,6 +933,12 @@
             collective_id=0, has_side_effects=True, vmem_limit_bytes=60 * 1024 * 1024
         ),
     )(keys, values, queries, positions, *operands)
+    return pl.pallas_call(
+        hand_out,
+        in_specs=[pl.BlockSpec(memory_space=pltpu.VMEM)],
+        out_specs=pl.BlockSpec(memory_space=pltpu.VMEM),
+        out_shape=jax.ShapeDtypeStruct(settled.shape, settled.dtype),
+    )(settled)
 
 
 def by_columns(keys, values, queries, positions):

time: 54.6 us -> 52.3 us (0.958)
  local copies, waits for them, and re-layouts: 1.77 us -> 0 us
  Pallas kernels: 52.7 us -> 52.1 us
    pallas_call x1, Pallas kernels: 52.7 us -> 50.3 us  [by_tokens(): pl.pallas_call(functools.partial(fused_kernel, count, math.log2(math.e) /...]
    unnamed x1 -> x0, local copies, waits for them, and re-layouts: 1.77 us -> none
    pallas_call x0 -> x1, Pallas kernels: none -> 1.77 us  [by_tokens(): pl.pallas_call(hand_out, in_specs=[pl.BlockSpec(memory_space=pltpu.VMEM)]...]
where the time goes in v7:
time: 52.3 us; the launch traced here: 52.1 us
  Pallas kernels  52.1 us (100%)
    pallas_call x1, Pallas kernels, by_tokens(): pl.pallas_call(functools.partial(fused_kernel, count, math.log2(math.e) /...  50.3 us
    pallas_call x1, Pallas kernels, by_tokens(): pl.pallas_call(hand_out, in_specs=[pl.BlockSpec(memory_space=pltpu.VMEM)]...  1.77 us

profile of v7, /device:TPU:0, one launch (start us, length us, event | category | flops | bytes accessed | tf_op | source)
XLA Modules:
  0.0 52.1 jit_solution(10591344134158770007)
XLA Ops:
  0.0 50.3 %shard_map.136.source_ref = bf16[2,768,128]{2,1,0:T(8,128)(2,1)} custom-call(bf16[4096,256]{1,0:T(8,128)(2,1)} %keys_hbm.1, bf16[4096,256]{1,0:T(8,128)(2,1)} %values_hbm.1, bf16[2,768,128]{2,1,0:T(8,128)(2,1)} %queries_hbm.1, s32[768]{0:T(1024)} %places_hbm.1, bf16[256,256]{1,0:T(8,128)(2,1)} %constant.20.clone.high_hbm, ...), custom_call_target="tpu_custom_call" | custom-call | tf_op jit(solution)/shard_map/pallas_call | solution.py:884
  50.3 1.8 %shard_map.137 = bf16[2,768,128]{2,1,0:T(8,128)(2,1)} custom-call(bf16[2,768,128]{2,1,0:T(8,128)(2,1)} %shard_map.136.source_ref), custom_call_target="tpu_custom_call" | custom-call | tf_op jit(solution)/shard_map/pallas_call | solution.py:936

commit v8 on v7

--- a/solution.py
+++ b/solution.py
@@ -331,7 +331,6 @@
     over_send,
     over_recv,
     last_send,
-    last_recv,
 ):
     me = lax.axis_index("ctx")
     heads, rows, width = queries_ref.shape
@@ -432,7 +431,7 @@
         return copy(
             asks_ref.at[source, head, here],
             asks_ref.at[source, head, here],
-            ask_send.at[source, head, block, side],
+            ask_send.at[source, side],
             ask_recv.at[source, head, block],
             me + 2 * side - 1,
         )
@@ -441,11 +440,6 @@
     for block in range(blocks):
         for_sides(lambda side: ask_copy(me, 0, block, side).start())
     for_sides(lambda side: greet(behind_sem.at[1 - side], me + 2 * side - 1))
-    for_sides(lambda side: pl.semaphore_wait(behind_sem.at[side], 1))
-
-    @pl.when(inside)
-    def _():
-        greet(end_sem, mate)
 
     for each in loads[4:6]:
         each.wait()
@@ -458,6 +452,13 @@
             parts_ref[
                 p * order : (p + 1) * order, side * half_columns : (side + 1) * half_columns
             ] = z[:order] + z[order:]
+        if p == 1:
+            for_sides(lambda side: pl.semaphore_wait(behind_sem.at[side], 1))
+
+            @pl.when(inside)
+            def _():
+                greet(end_sem, mate)
+
     whole_ref[...] = strict_dot(merge_ref[...], parts_ref[...])
     others_ref[:EDGE] = whole_ref[pl.ds(pl.multiple_of(jnp.where(lower, 0, EDGE), EDGE), EDGE), :]
 
@@ -498,6 +499,15 @@
             field_recv.at[source],
             source,
         ).wait_recv()
+
+    def ask_sent(source, side):
+        copy(
+            asks_ref.at[source],
+            asks_ref.at[source],
+            ask_send.at[source, side],
+            ask_recv.at[source, 0, 0],
+            me + 2 * side - 1,
+        ).wait_send()
 
     def hand(source, head, block, side):
         handed = ask_copy(source, head, block, side)
@@ -591,16 +601,16 @@
         (0, 0, 0, blocks),
         (1, 0, 0, blocks),
         (2, 0, 0, blocks),
-        (0, 1, 0, blocks - 1),
+        (3, 0, 0, blocks - 1),
         (2, 1, 0, blocks),
-        (3, 0, 0, blocks - 1),
+        (3, 0, blocks - 1, 1),
+        (3, 1, 0, 1),
         (1, 1, 0, blocks),
-        (0, 1, blocks - 1, 1),
-        (3, 0, blocks - 1, 1),
-        (3, 1, 0, blocks),
+        (0, 1, 0, blocks),
+        (3, 1, 1, blocks - 1),
     ]
     begins = [sum(run[3] for run in runs[:i]) for i in range(len(runs))]
-    units = begins[-1] + blocks
+    units = begins[-1] + runs[-1][3]
 
     def decode(u):
         kind, head, block = runs[0][0], runs[0][1], u
@@ -659,7 +669,7 @@
             own_log_ref.at[at],
             half_ref.at[at],
             half_log_ref.at[at],
-            half_send.at[at],
+            half_send,
             half_recv.at[at],
             mate,
         )
@@ -671,7 +681,7 @@
             merged_log_ref.at[at],
             over_ref.at[at],
             over_log_ref.at[at],
-            over_send.at[at],
+            over_send,
             over_recv.at[at],
             near_over,
         )
@@ -683,8 +693,8 @@
             ready_log_ref.at[at],
             last_ref.at[at],
             last_log_ref.at[at],
-            last_send.at[at],
-            last_recv.at[at],
+            last_send,
+            half_recv.at[(0,) + at],
             mate,
         )
 
@@ -738,8 +748,7 @@
         def _():
             ask_copy(source, head, block, 1 - outward).wait_recv()
 
-    merges = ((1, 0, begins[1] + 7), (2, 0, begins[2] + 8), (2, 1, begins[4] + 8))
-    passes = begins[2] + 12
+    merges = ((1, 0, begins[1] + 9), (2, 0, begins[2] + 12))
 
     def send_on(u):
         kind, head, block, _ = decode(u)
@@ -755,12 +764,6 @@
             @pl.when(jnp.logical_and(inside, jnp.logical_and(k >= 0, k < blocks)))
             def _():
                 merge_half(kind, head, k)
-
-        k = u - passes
-
-        @pl.when(jnp.logical_and(inside, jnp.logical_and(k >= 0, k < blocks)))
-        def _():
-            pass_on(0, k)
 
     await_ask(jnp.int32(0))
     score(jnp.int32(0), even_ref, even_top_ref)
@@ -797,17 +800,16 @@
     @pl.when(inside)
     def _():
         for block in range(blocks):
+            pass_on(0, block)
+            merge_half(2, 1, block)
+        for block in range(blocks):
             pass_on(1, block)
             merge_half(1, 1, block)
-        for head in range(heads):
-            for block in range(blocks):
-                ask_copy(me - 1, head, block, 1).wait_send()
-                ask_copy(me + 1, head, block, 0).wait_send()
-                ask_copy(far_end, head, block, outward).wait_send()
-
-    for head in range(heads):
-        for block in range(blocks):
-            for_sides(lambda side: ask_copy(me, head, block, side).wait_send())
+        ask_sent(me - 1, 1)
+        ask_sent(me + 1, 0)
+        ask_sent(far_end, outward)
+
+    for_sides(lambda side: ask_sent(me, side))
     for_sides(lambda side: near_copy(side).wait_send())
     for_far(lambda other: far_copy(other).wait_send())
 
@@ -816,18 +818,13 @@
         for head in range(heads):
             for block in range(blocks):
                 settle(head, block)
-        for head in range(heads):
-            for block in range(blocks):
-                for each in over_copy(0, head, block) + over_copy(1, head, block) + last_copy(head, block):
-                    each.wait_send()
+        for each in both(
+            merged_ref, merged_log_ref, over_ref, over_log_ref, over_send, over_recv.at[0, 0, 0], near_over
+        ) + both(ready_ref, ready_log_ref, last_ref, last_log_ref, last_send, half_recv.at[0, 0, 0], mate):
+            each.wait_send()
 
     @pl.when(jnp.logical_not(inside))
     def _():
-        for kind in range(3):
-            for head in range(heads):
-                for block in range(blocks):
-                    for each in half_copy(kind, head, block):
-                        each.wait_send()
         for head in range(heads):
             for block in range(blocks):
                 for each in last_copy(head, block):
@@ -837,10 +834,11 @@
                     [own_log_ref[3, head, block], last_log_ref[head, block]],
                 )
                 out_ref[head, block * BLOCK : (block + 1) * BLOCK, :] = mixed.T.astype(out_ref.dtype)
-
-
-def hand_out(source_ref, out_ref):
-    out_ref[...] = source_ref[...]
+        kinds = pl.ds(0, 3)
+        for each in both(
+            own_ref.at[kinds], own_log_ref.at[kinds], half_ref, half_log_ref, half_send, half_recv.at[0, 0, 0], mate
+        ):
+            each.wait_send()
 
 
 def by_tokens(keys, values, queries, positions, count):
@@ -881,7 +879,7 @@
             pltpu.VMEM(lead + (heads, blocks, 1, BLOCK), jnp.float32),
         ]
 
-    settled = pl.pallas_call(
+    return pl.pallas_call(
         functools.partial(fused_kernel, count, math.log2(math.e) / math.sqrt(width)),
         in_specs=[pl.BlockSpec(memory_space=pl.ANY)] * 14,
         out_specs=pl.BlockSpec(memory_space=pltpu.VMEM),
@@ -920,25 +918,18 @@
             pltpu.SemaphoreType.REGULAR,
             dma((count,)),
             dma((count,)),
-            dma((count, heads, blocks, 2)),
+            dma((count, 2)),
             dma((count, heads, blocks)),
+            dma((2,)),
             dma((3, heads, blocks, 2)),
-            dma((3, heads, blocks, 2)),
+            dma((2,)),
             dma((2, heads, blocks, 2)),
-            dma((2, heads, blocks, 2)),
-            dma((heads, blocks, 2)),
-            dma((heads, blocks, 2)),
+            dma((2,)),
         ],
         compiler_params=pltpu.CompilerParams(
             collective_id=0, has_side_effects=True, vmem_limit_bytes=60 * 1024 * 1024
         ),
     )(keys, values, queries, positions, *operands)
-    return pl.pallas_call(
-        hand_out,
-        in_specs=[pl.BlockSpec(memory_space=pltpu.VMEM)],
-        out_specs=pl.BlockSpec(memory_space=pltpu.VMEM),
-        out_shape=jax.ShapeDtypeStruct(settled.shape, settled.dtype),
-    )(settled)
 
 
 def by_columns(keys, values, queries, positions):

time: 52.3 us -> 51.4 us (0.983)
  Pallas kernels: 52.1 us -> 49.4 us
  local copies, waits for them, and re-layouts: 0 us -> 1.77 us
    unnamed x0 -> x1, local copies, waits for them, and re-layouts: none -> 1.77 us
    pallas_call x1 -> x0, Pallas kernels: 1.77 us -> none  [by_tokens(): pl.pallas_call(hand_out, in_specs=[pl.BlockSpec(memory_space=pltpu.VMEM)]...]
    pallas_call x1, Pallas kernels: 50.3 us -> 49.4 us  [by_tokens(): pl.pallas_call(functools.partial(fused_kernel, count, math.log2(math.e) /...]
where the time goes in v8:
time: 51.4 us; the launch traced here: 51.2 us
  Pallas kernels  49.4 us (96%)
  local copies, waits for them, and re-layouts  1.77 us (3%)
    pallas_call x1, Pallas kernels, by_tokens(): pl.pallas_call(functools.partial(fused_kernel, count, math.log2(math.e) /...  49.4 us
    unnamed x1, local copies, waits for them, and re-layouts  1.77 us

profile of v8, /device:TPU:0, one launch (start us, length us, event | category | flops | bytes accessed | tf_op | source)
XLA Modules:
  0.0 51.2 jit_solution(13625239344516736963)
XLA Ops:
  0.0 49.4 %shard_map.136 = bf16[2,768,128]{2,1,0:T(8,128)(2,1)} custom-call(bf16[4096,256]{1,0:T(8,128)(2,1)} %keys_hbm.1, bf16[4096,256]{1,0:T(8,128)(2,1)} %values_hbm.1, bf16[2,768,128]{2,1,0:T(8,128)(2,1)} %queries_hbm.1, s32[768]{0:T(1024)} %places_hbm.1, bf16[256,256]{1,0:T(8,128)(2,1)} %constant.20.clone.high_hbm, bf16[256,256]{1,0:T(8,128)(2,1)} %constant.21.clone.low_hbm, ...), custom_call_target="tpu_custom_call" | custom-call | tf_op jit(solution)/shard_map/pallas_call | solution.py:882
  49.4 1.8 %copy.16 = bf16[2,768,128]{2,1,0:T(8,128)(2,1)} copy(bf16[2,768,128]{2,1,0:T(8,128)(2,1)} %shard_map.136) | data formatting | bytes 786432

commit v9 on v8

--- a/solution.py
+++ b/solution.py
@@ -13,7 +13,7 @@
 PARTS = 4
 ORDER = 64
 EDGE = 32
-FAR = 16
+FAR = 8
 BLOCK = 256
 MESH = pl.DeviceIdType.MESH
 
@@ -437,7 +437,7 @@
         )
 
     pl.semaphore_wait(barrier, jnp.where(inside, 2, 1))
-    for block in range(blocks):
+    for block in range(blocks - 1):
         for_sides(lambda side: ask_copy(me, 0, block, side).start())
     for_sides(lambda side: greet(behind_sem.at[1 - side], me + 2 * side - 1))
 
@@ -521,13 +521,13 @@
             def _():
                 action(other)
 
-    for_sides(lambda side: near_copy(side).start())
-
     @pl.when(jnp.logical_not(inside))
     def _():
         pl.semaphore_wait(end_sem, 1)
 
     for_far(lambda other: far_copy(other).start())
+    for_sides(lambda side: near_copy(side).start())
+    for_sides(lambda side: ask_copy(me, 0, blocks - 1, side).start())
 
     @pl.when(jnp.logical_not(inside))
     def _():
@@ -567,28 +567,33 @@
     for_far(far_wait)
     field_ref[...] += strict_dot(cross_ref[...], others_ref[...])
 
-    def finish(p, carry):
-        f = field_ref[pl.ds(pl.multiple_of(p * order, order), order), :]
-        high = f.astype(jnp.bfloat16)
-        low = (f - high.astype(jnp.float32)).astype(jnp.bfloat16)
-        y = close_ref[p] + jnp.dot(
-            up_ref[...], jnp.concatenate([high, low, high], axis=0), preferred_element_type=jnp.float32
-        )
-        y = y.astype(jnp.bfloat16).astype(jnp.float32)
-        begin = pl.multiple_of(p * t_part, t_part)
-        place = me * PARTS + p
-        cos_p, sin_p = coarse_ref[0, pl.ds(place, 1), :], coarse_ref[1, pl.ds(place, 1), :]
-        cosine = cos_p * fine_ref[0] - sin_p * fine_ref[1]
-        sine = sin_p * fine_ref[0] + cos_p * fine_ref[1]
-        for head in range(heads):
-            k = y[:, head * width : (head + 1) * width]
+    def finish(head):
+        k_columns = slice(head * width, (head + 1) * width)
+        v_columns = slice(half_columns + head * width, half_columns + (head + 1) * width)
+
+        def one(p, carry):
+            at = pl.ds(pl.multiple_of(p * order, order), order)
+            f = jnp.concatenate([field_ref[at, k_columns], field_ref[at, v_columns]], axis=1)
+            high = f.astype(jnp.bfloat16)
+            low = (f - high.astype(jnp.float32)).astype(jnp.bfloat16)
+            y = jnp.dot(
+                up_ref[...], jnp.concatenate([high, low, high], axis=0), preferred_element_type=jnp.float32
+            )
+            k = (close_ref[p, :, k_columns] + y[:, :width]).astype(jnp.bfloat16).astype(jnp.float32)
+            v = (close_ref[p, :, v_columns] + y[:, width:]).astype(jnp.bfloat16).astype(jnp.float32)
+            begin = pl.multiple_of(p * t_part, t_part)
+            place = me * PARTS + p
+            cos_p, sin_p = coarse_ref[0, pl.ds(place, 1), :], coarse_ref[1, pl.ds(place, 1), :]
+            cosine = cos_p * fine_ref[0] - sin_p * fine_ref[1]
+            sine = sin_p * fine_ref[0] + cos_p * fine_ref[1]
             turned = k * cosine + pltpu.roll(k, width // 2, 1) * sine
             k_ref[head, pl.ds(begin, t_part), :] = turned.astype(jnp.bfloat16)
-            v = y[:, half_columns + head * width : half_columns + (head + 1) * width]
             v_ref[head, :, pl.ds(begin, t_part)] = v.T.astype(jnp.bfloat16)
-        return carry
-
-    lax.fori_loop(0, PARTS, finish, 0)
+            return carry
+
+        lax.fori_loop(0, PARTS, one, 0)
+
+    finish(0)
 
     @pl.when(inside)
     def _():
@@ -779,6 +784,10 @@
                 if source is near_over:
                     for block in range(2, blocks):
                         ask_copy(me, 1, block, outward).start()
+
+        @pl.when(i == 2)
+        def _():
+            finish(1)
 
         await_ask(u + 1)
         score(u + 1, odd_ref, odd_top_ref)

time: 51.4 us -> 54.2 us (1.054)
  Pallas kernels: 49.4 us -> 52.3 us
    pallas_call x1, Pallas kernels: 49.4 us -> 52.3 us  [by_tokens(): pl.pallas_call(functools.partial(fused_kernel, count, math.log2(math.e) /...]
where the time goes in v9:
time: 54.2 us; the launch traced here: 54 us
  Pallas kernels  52.3 us (96%)
  local copies, waits for them, and re-layouts  1.77 us (3%)
    pallas_call x1, Pallas kernels, by_tokens(): pl.pallas_call(functools.partial(fused_kernel, count, math.log2(math.e) /...  52.3 us
    unnamed x1, local copies, waits for them, and re-layouts  1.77 us

profile of v9, /device:TPU:0, one launch (start us, length us, event | category | flops | bytes accessed | tf_op | source)
XLA Modules:
  0.0 54.0 jit_solution(5987163707351679942)
XLA Ops:
  0.0 52.3 %shard_map.136 = bf16[2,768,128]{2,1,0:T(8,128)(2,1)} custom-call(bf16[4096,256]{1,0:T(8,128)(2,1)} %keys_hbm.1, bf16[4096,256]{1,0:T(8,128)(2,1)} %values_hbm.1, bf16[2,768,128]{2,1,0:T(8,128)(2,1)} %queries_hbm.1, s32[768]{0:T(1024)} %places_hbm.1, bf16[256,256]{1,0:T(8,128)(2,1)} %constant.20.clone.high_hbm, bf16[256,256]{1,0:T(8,128)(2,1)} %constant.21.clone.low_hbm, ...), custom_call_target="tpu_custom_call" | custom-call | tf_op jit(solution)/shard_map/pallas_call | solution.py:891
  52.3 1.8 %copy.16 = bf16[2,768,128]{2,1,0:T(8,128)(2,1)} copy(bf16[2,768,128]{2,1,0:T(8,128)(2,1)} %shard_map.136) | data formatting | bytes 786432

commit v10 on v9

--- a/solution.py
+++ b/solution.py
@@ -547,7 +547,7 @@
 
     @pl.when(inside)
     def _():
-        for block in range(blocks):
+        for block in range(blocks - 1):
             for side in range(2):
                 hand(me + 2 * side - 1, 0, block, 1 - side)
         ask_copy(me, 1, 0, outward).start()
@@ -556,6 +556,8 @@
 
     @pl.when(inside)
     def _():
+        for side in range(2):
+            hand(me + 2 * side - 1, 0, blocks - 1, 1 - side)
         hand(mate, 1, 0, 1 - outward)
         ask_copy(me, 1, 1, outward).start()
 

time: 54.2 us -> 51.9 us (0.958)
  Pallas kernels: 52.3 us -> 50 us
    pallas_call x1, Pallas kernels: 52.3 us -> 50 us  [by_tokens(): pl.pallas_call(functools.partial(fused_kernel, count, math.log2(math.e) /...]
where the time goes in v10:
time: 51.9 us; the launch traced here: 51.8 us
  Pallas kernels  50 us (96%)
  local copies, waits for them, and re-layouts  1.77 us (3%)
    pallas_call x1, Pallas kernels, by_tokens(): pl.pallas_call(functools.partial(fused_kernel, count, math.log2(math.e) /...  50 us
    unnamed x1, local copies, waits for them, and re-layouts  1.77 us

profile of v10, /device:TPU:0, one launch (start us, length us, event | category | flops | bytes accessed | tf_op | source)
XLA Modules:
  0.0 51.8 jit_solution(2772836239579270664)
XLA Ops:
  0.0 50.0 %shard_map.136 = bf16[2,768,128]{2,1,0:T(8,128)(2,1)} custom-call(bf16[4096,256]{1,0:T(8,128)(2,1)} %keys_hbm.1, bf16[4096,256]{1,0:T(8,128)(2,1)} %values_hbm.1, bf16[2,768,128]{2,1,0:T(8,128)(2,1)} %queries_hbm.1, s32[768]{0:T(1024)} %places_hbm.1, bf16[256,256]{1,0:T(8,128)(2,1)} %constant.20.clone.high_hbm, bf16[256,256]{1,0:T(8,128)(2,1)} %constant.21.clone.low_hbm, ...), custom_call_target="tpu_custom_call" | custom-call | tf_op jit(solution)/shard_map/pallas_call | solution.py:893
  50.0 1.8 %copy.16 = bf16[2,768,128]{2,1,0:T(8,128)(2,1)} copy(bf16[2,768,128]{2,1,0:T(8,128)(2,1)} %shard_map.136) | data formatting | bytes 786432

commit v11 on v10

--- a/solution.py
+++ b/solution.py
@@ -755,7 +755,8 @@
         def _():
             ask_copy(source, head, block, 1 - outward).wait_recv()
 
-    merges = ((1, 0, begins[1] + 9), (2, 0, begins[2] + 12))
+    merges = ((1, 0, begins[1] + 5), (2, 0, begins[2] + 7), (2, 1, begins[4] + 8))
+    passes = begins[4] + 8
 
     def send_on(u):
         kind, head, block, _ = decode(u)
@@ -764,6 +765,12 @@
         def _():
             for each in half_copy(kind, head, block):
                 each.start()
+
+        k_pass = u - passes
+
+        @pl.when(jnp.logical_and(inside, jnp.logical_and(k_pass >= 0, k_pass < blocks)))
+        def _():
+            pass_on(0, k_pass)
 
         for kind, head, first in merges:
             k = u - first
@@ -810,9 +817,6 @@
 
     @pl.when(inside)
     def _():
-        for block in range(blocks):
-            pass_on(0, block)
-            merge_half(2, 1, block)
         for block in range(blocks):
             pass_on(1, block)
             merge_half(1, 1, block)

time: 51.9 us -> 49.1 us (0.946)
  Pallas kernels: 50 us -> 47.2 us
    pallas_call x1, Pallas kernels: 50 us -> 47.2 us  [by_tokens(): pl.pallas_call(functools.partial(fused_kernel, count, math.log2(math.e) /...]
where the time goes in v11:
time: 49.1 us; the launch traced here: 49 us
  Pallas kernels  47.2 us (96%)
  local copies, waits for them, and re-layouts  1.77 us (4%)
    pallas_call x1, Pallas kernels, by_tokens(): pl.pallas_call(functools.partial(fused_kernel, count, math.log2(math.e) /...  47.2 us
    unnamed x1, local copies, waits for them, and re-layouts  1.77 us

profile of v11, /device:TPU:0, one launch (start us, length us, event | category | flops | bytes accessed | tf_op | source)
XLA Modules:
  0.0 49.0 jit_solution(7368367447633095174)
XLA Ops:
  0.0 47.2 %shard_map.136 = bf16[2,768,128]{2,1,0:T(8,128)(2,1)} custom-call(bf16[4096,256]{1,0:T(8,128)(2,1)} %keys_hbm.1, bf16[4096,256]{1,0:T(8,128)(2,1)} %values_hbm.1, bf16[2,768,128]{2,1,0:T(8,128)(2,1)} %queries_hbm.1, s32[768]{0:T(1024)} %places_hbm.1, bf16[256,256]{1,0:T(8,128)(2,1)} %constant.20.clone.high_hbm, bf16[256,256]{1,0:T(8,128)(2,1)} %constant.21.clone.low_hbm, ...), custom_call_target="tpu_custom_call" | custom-call | tf_op jit(solution)/shard_map/pallas_call | solution.py:897
  47.2 1.8 %copy.16 = bf16[2,768,128]{2,1,0:T(8,128)(2,1)} copy(bf16[2,768,128]{2,1,0:T(8,128)(2,1)} %shard_map.136) | data formatting | bytes 786432

commit v12 on v11

--- a/solution.py
+++ b/solution.py
@@ -755,8 +755,8 @@
         def _():
             ask_copy(source, head, block, 1 - outward).wait_recv()
 
-    merges = ((1, 0, begins[1] + 5), (2, 0, begins[2] + 7), (2, 1, begins[4] + 8))
-    passes = begins[4] + 8
+    merges = ((1, 0, begins[1] + 3), (2, 0, begins[2] + 5), (2, 1, begins[4] + 6))
+    passes = begins[4] + 7
 
     def send_on(u):
         kind, head, block, _ = decode(u)

time: 49.1 us -> 47.6 us (0.969)
  Pallas kernels: 47.2 us -> 45.7 us
    pallas_call x1, Pallas kernels: 47.2 us -> 45.7 us  [by_tokens(): pl.pallas_call(functools.partial(fused_kernel, count, math.log2(math.e) /...]
where the time goes in v12:
time: 47.6 us; the launch traced here: 47.5 us
  Pallas kernels  45.7 us (96%)
  local copies, waits for them, and re-layouts  1.77 us (4%)
    pallas_call x1, Pallas kernels, by_tokens(): pl.pallas_call(functools.partial(fused_kernel, count, math.log2(math.e) /...  45.7 us
    unnamed x1, local copies, waits for them, and re-layouts  1.77 us

profile of v12, /device:TPU:0, one launch (start us, length us, event | category | flops | bytes accessed | tf_op | source)
XLA Modules:
  0.0 47.5 jit_solution(11970239640187166667)
XLA Ops:
  0.0 45.7 %shard_map.136 = bf16[2,768,128]{2,1,0:T(8,128)(2,1)} custom-call(bf16[4096,256]{1,0:T(8,128)(2,1)} %keys_hbm.1, bf16[4096,256]{1,0:T(8,128)(2,1)} %values_hbm.1, bf16[2,768,128]{2,1,0:T(8,128)(2,1)} %queries_hbm.1, s32[768]{0:T(1024)} %places_hbm.1, bf16[256,256]{1,0:T(8,128)(2,1)} %constant.20.clone.high_hbm, bf16[256,256]{1,0:T(8,128)(2,1)} %constant.21.clone.low_hbm, ...), custom_call_target="tpu_custom_call" | custom-call | tf_op jit(solution)/shard_map/pallas_call | solution.py:897
  45.7 1.8 %copy.16 = bf16[2,768,128]{2,1,0:T(8,128)(2,1)} copy(bf16[2,768,128]{2,1,0:T(8,128)(2,1)} %shard_map.136) | data formatting | bytes 786432

commit v13 on v12

--- a/solution.py
+++ b/solution.py
@@ -755,8 +755,8 @@
         def _():
             ask_copy(source, head, block, 1 - outward).wait_recv()
 
-    merges = ((1, 0, begins[1] + 3), (2, 0, begins[2] + 5), (2, 1, begins[4] + 6))
-    passes = begins[4] + 7
+    merges = ((1, 0, begins[1] + 3), (2, 0, begins[2] + 4), (2, 1, begins[4] + 5))
+    passes = begins[4] + 6
 
     def send_on(u):
         kind, head, block, _ = decode(u)

time: 47.6 us -> 48.1 us (1.011)
  no operation moved by 1% of the time
where the time goes in v13:
time: 48.1 us; the launch traced here: 47.9 us
  Pallas kernels  46.1 us (96%)
  local copies, waits for them, and re-layouts  1.77 us (4%)
    pallas_call x1, Pallas kernels, by_tokens(): pl.pallas_call(functools.partial(fused_kernel, count, math.log2(math.e) /...  46.1 us
    unnamed x1, local copies, waits for them, and re-layouts  1.77 us

profile of v13, /device:TPU:0, one launch (start us, length us, event | category | flops | bytes accessed | tf_op | source)
XLA Modules:
  0.0 47.9 jit_solution(9060507001757118919)
XLA Ops:
  0.0 46.1 %shard_map.136 = bf16[2,768,128]{2,1,0:T(8,128)(2,1)} custom-call(bf16[4096,256]{1,0:T(8,128)(2,1)} %keys_hbm.1, bf16[4096,256]{1,0:T(8,128)(2,1)} %values_hbm.1, bf16[2,768,128]{2,1,0:T(8,128)(2,1)} %queries_hbm.1, s32[768]{0:T(1024)} %places_hbm.1, bf16[256,256]{1,0:T(8,128)(2,1)} %constant.20.clone.high_hbm, bf16[256,256]{1,0:T(8,128)(2,1)} %constant.21.clone.low_hbm, ...), custom_call_target="tpu_custom_call" | custom-call | tf_op jit(solution)/shard_map/pallas_call | solution.py:897
  46.1 1.8 %copy.16 = bf16[2,768,128]{2,1,0:T(8,128)(2,1)} copy(bf16[2,768,128]{2,1,0:T(8,128)(2,1)} %shard_map.136) | data formatting | bytes 786432
